TPU v7x, 32 devices: a whole 2x2x4 slice. The times are simulated.
32 devices in a mesh: tm: 4 (over x, core), rows: 8 (over z, y).
Axes of the slice: x: 2, y: 2, z: 4, core: 2. Of those that a mesh axis runs over, the one named last changes fastest.
Arguments:
- latent: bfloat16 [8, 16, 160, 16], P('tm', 'rows'), may hold values from -6 to 6
- entry_kernel: bfloat16 [3, 3, 3, 16, 256], replicated, may hold values from -0.3125 to 0.3125
- middle_kernel: bfloat16 [3, 3, 3, 256, 256], replicated, may hold values from -0.078125 to 0.078125
- upper_kernel: bfloat16 [3, 3, 3, 256, 256], replicated, may hold values from -0.078125 to 0.078125
Outputs:
- decoded: bfloat16 [8, 32, 320, 256], P('tm', 'rows')
All inputs are finite; a program needn't handle non-finite values.
Results may differ from a plain program's by a relative error of at most 0.0059.
Values may be sent and summed in bfloat16 or wider, within the bound.
No kernel may reach another device: no remote copies, remote signals or barrier semaphores. Data moves between devices by JAX's collectives and lax.ppermute only.
A program may use at most 64 MiB of HBM per device.

v0:
```python
import jax
import jax.numpy as jnp
from jax import lax
from jax.sharding import PartitionSpec as P


def shifted(block, axis, distance):
    devices = range(lax.axis_size(axis))
    route = [(i - distance, i) for i in devices if i - distance in devices]
    return lax.ppermute(block, axis, route)


def with_halo(array, sides, width):
    for axis, dim in sides:
        size, length = (lax.axis_size(axis), array.shape[dim])
        up = [(i, (i + 1) % size) for i in range(size - 1)]
        down = [(j, i) for i, j in up]
        last = lax.slice_in_dim(array, length - width, length, axis=dim)
        first = lax.slice_in_dim(array, 0, width, axis=dim)
        before = lax.ppermute(last, axis, up)
        after = lax.ppermute(first, axis, down)
        array = jnp.concatenate([before, array, after], axis=dim)
    return array


def convolve(field, weight):
    padded = jnp.pad(field, ((0, 0), (0, 0), (1, 1), (0, 0)))
    result = lax.conv_general_dilated(
        padded[None],
        weight,
        (1, 1, 1),
        "VALID",
        dimension_numbers=("NDHWC", "DHWIO", "NDHWC"),
        preferred_element_type=jnp.float32,
    )
    return result[0]


def per_device(latent, entry_kernel, middle_kernel, upper_kernel):
    frames = latent.shape[0]
    height = latent.shape[1]
    nearer = shifted(latent, "tm", 1)
    farther = shifted(latent, "tm", 2)
    nearer = jnp.concatenate([farther, nearer], 0)
    stretched = jnp.concatenate([nearer, latent], 0)
    rimmed = with_halo(stretched, (("rows", 1),), 2)
    entry = convolve(rimmed, entry_kernel)
    first_row = lax.axis_index("rows") * height - 1
    row_index = first_row + jnp.arange(height + 2, dtype=jnp.int32)
    inside = ((row_index >= 0) & (row_index < height * lax.axis_size("rows"))).astype(jnp.float32)
    widened = (entry * inside[None, :, None, None]).astype(jnp.bfloat16)
    bottom = widened[2:, 1 : height + 1]
    middle = convolve(widened, middle_kernel)
    section_one = (bottom.astype(jnp.float32) + jax.nn.silu(middle)).astype(jnp.bfloat16)
    preceding = shifted(section_one[frames - 2 :], "tm", 1)
    bordered = with_halo(jnp.concatenate([preceding, section_one], 0), (("rows", 1),), 1)
    enlarged = jnp.repeat(jnp.repeat(bordered, 2, axis=1), 2, axis=2)[:, 1:-1]
    return jax.nn.silu(convolve(enlarged, upper_kernel)).astype(jnp.bfloat16)


def solution(mesh):
    return jax.shard_map(
        per_device,
        mesh=mesh,
        in_specs=(P("tm", "rows", None, None), P(), P(), P()),
        out_specs=P("tm", "rows", None, None),
        check_vma=False,
    )
```

profile of v0, /device:TPU:0, one launch (start us, length us, event | category | flops | bytes accessed | tf_op | source)
XLA Modules:
  0.0 92.7 jit_solution(160538245140628578)
XLA Ops:
  0.0 5.7 %collective-permute-start = (bf16[2,2,160,16]{2,3,1,0:T(8,128)(2,1)}, bf16[2,2,160,16]{2,3,1,0:T(8,128)(2,1)}, u32[]{:S(2)}, u32[]{:S(2)}) collective-permute-start(bf16[2,2,160,16]{2,3,1,0:T(8,128)(2,1)} %param.4), channel_id=1, source_target_pairs={{0,16},{8,24},{1,17},{9,25},{2,18},{10,26},{3,19},{11,27},{4,20},{... | collective-permute-start | bytes 61448 | tf_op jit(solution)/shard_map/ppermute | solution.py:10
  5.7 2.1 %collective-permute-start.1 = (bf16[2,2,160,16]{2,3,1,0:T(8,128)(2,1)}, bf16[2,2,160,16]{2,3,1,0:T(8,128)(2,1)}, u32[]{:S(2)}, u32[]{:S(2)}) collective-permute-start(bf16[2,2,160,16]{2,3,1,0:T(8,128)(2,1)} %param.4), channel_id=1, source_target_pairs={{0,8},{8,16},{16,24},{1,9},{9,17},{17,25},{2,10},{10,18},{18,26},{... | collective-permute-start | bytes 61448 | tf_op jit(solution)/shard_map/ppermute | solution.py:10
  7.8 0.8 constant_dynamic-update-slice_fusion.2
  8.6 0.8 constant_dynamic-update-slice_fusion.1
  9.3 0.8 constant_dynamic-update-slice_fusion
  10.1 1.3 %collective-permute-start.3 = (bf16[6,2,160,16]{2,3,1,0:T(8,128)(2,1)S(1)}, bf16[6,2,160,16]{2,3,1,0:T(8,128)(2,1)S(1)}, u32[]{:S(2)}, u32[]{:S(2)}) collective-permute-start(bf16[6,2,160,16]{2,3,1,0:T(8,128)(2,1)S(1)} %constant_dynamic-update-slice_fusion), channel_id=1, source_target_pairs={{1,0},{2,1},{3,2},{4,3},{5,4},{6,5},{7,6},{9,8},{10,9},{11,10},{12... | collective-permute-start | bytes 184328 | tf_op jit(solution)/shard_map/ppermute | solution.py:21
  11.4 4.6 %collective-permute-start.2 = (bf16[6,2,160,16]{2,3,1,0:T(8,128)(2,1)S(1)}, bf16[6,2,160,16]{2,3,1,0:T(8,128)(2,1)S(1)}, u32[]{:S(2)}, u32[]{:S(2)}) collective-permute-start(bf16[6,2,160,16]{2,3,1,0:T(8,128)(2,1)S(1)} %constant_dynamic-update-slice_fusion), channel_id=1, source_target_pairs={{0,1},{1,2},{2,3},{3,4},{4,5},{5,6},{6,7},{8,9},{9,10},{10,11},{11... | collective-permute-start | bytes 184328 | tf_op jit(solution)/shard_map/ppermute | solution.py:20
  15.9 0.9 collective-permute-done.3
  16.8 2.0 %collective-permute-done.2 = bf16[6,2,160,16]{2,3,1,0:T(8,128)(2,1)S(1)} collective-permute-done((bf16[6,2,160,16]{2,3,1,0:T(8,128)(2,1)S(1)}, bf16[6,2,160,16]{2,3,1,0:T(8,128)(2,1)S(1)}, u32[]{:S(2)}, u32[]{:S(2)}) %collective-permute-start.2) | collective-permute-done | bytes 61472 | tf_op jit(solution)/shard_map/ppermute | solution.py:20
  18.9 0.2 fusion.46
  19.1 0.8 pad.15
  19.8 2.6 %reshape.18 = bf16[6,6,1,8,21,16]{4,3,5,1,0,2:T(8,128)(2,1)} reshape(bf16[6,6,1,168,16]{3,4,1,0,2:T(8,128)(2,1)} %pad.15) | data formatting | bytes 387072 | tf_op jit(solution)/shard_map/conv_general_dilated | solution.py:28
  22.4 4.1 %copy.32 = bf16[6,6,1,8,21,16]{5,3,4,1,0,2:T(8,128)(2,1)} copy(bf16[6,6,1,8,21,16]{4,3,5,1,0,2:T(8,128)(2,1)} %reshape.18) | data formatting | bytes 387072 | tf_op jit(solution)/shard_map/conv_general_dilated | solution.py:28
  26.5 1.0 %slice.22 = bf16[6,6,1,7,2,16]{5,3,4,1,0,2:T(8,128)(2,1)S(1)} slice(bf16[6,6,1,8,21,16]{5,3,4,1,0,2:T(8,128)(2,1)} %copy.32), slice={[0:6], [0:6], [0:1], [1:8], [0:2], [0:16]} | slice | bytes 32256 | tf_op jit(solution)/shard_map/conv_general_dilated | solution.py:28
  27.5 3.6 %fusion.20 = f32[4,4,8,21,256]{4,2,3,1,0:T(8,128)S(1)} fusion(bf16[3,3,3,16,256]{4,3,2,1,0:T(8,128)(2,1)} %param.5, bf16[6,6,1,7,2,16]{5,3,4,1,0,2:T(8,128)(2,1)S(1)} %slice.22, bf16[6,6,1,8,21,16]{5,3,4,1,0,2:T(8,128)(2,1)} %copy.32, pred[8,21]{0,1:T(8,128)(4,1)S(1)} %copy-done.3), kind=kOutput, calls=%fused_computation.25 | convolution fusion | flops 595866624 | bytes 3183528 | tf_op jit(solution)/shard_map/conv_general_dilated | solution.py:28
  31.1 1.1 %copy.33 = f32[4,4,8,21,256]{4,1,3,2,0:T(4,128)S(1)} copy(f32[4,4,8,21,256]{4,2,3,1,0:T(8,128)S(1)} %fusion.20) | data formatting | bytes 5505024 | tf_op jit(solution)/shard_map/conv_general_dilated | solution.py:28
  32.2 0.5 fusion.11
  32.7 0.6 pad_bitcast_fusion.1
  33.3 0.5 pad.17
  33.8 0.2 copy.35
  34.0 1.2 %copy-done.1 = bf16[3,3,3,256,256]{4,3,2,1,0:T(8,128)(2,1)S(1)} copy-done((bf16[3,3,3,256,256]{4,3,2,1,0:T(8,128)(2,1)S(1)}, bf16[3,3,3,256,256]{4,3,2,1,0:T(8,128)(2,1)}, u32[]{:S(2)}) %copy-start.1) | copy-done | bytes 3538968
  35.3 2.6 %fusion.33 = f32[2,2,8,21,256]{4,2,3,1,0:T(8,128)S(1)} fusion(bf16[3,3,3,256,256]{4,3,2,1,0:T(8,128)(2,1)S(1)} %copy-done.1, bf16[4,4,1,7,2,256]{5,3,4,1,0,2:T(8,128)(2,1)S(1)} %slice.25, bf16[4,4,1,8,21,256]{5,3,4,1,0,2:T(8,128)(2,1)S(1)} %copy.35, pred[8,21]{0,1:T(8,128)(4,1)S(1)} %copy-done.3), kind=kOutput, calls=%fused_computation.35 | convolution fusion | flops 2382864384 | bytes 5718184 | tf_op jit(solution)/shard_map/conv_general_dilated | solution.py:28
  37.9 0.4 copy.36
  38.3 0.9 fusion.39
  39.1 1.8 %collective-permute-start.4 = (bf16[2,2,160,256]{3,1,2,0:T(2,128)(2,1)S(1)}, bf16[2,2,160,256]{3,1,2,0:T(2,128)(2,1)S(1)}, u32[]{:S(2)}, u32[]{:S(2)}) collective-permute-start(bf16[2,2,160,256]{3,1,2,0:T(2,128)(2,1)S(1)} %fusion.39), channel_id=1, source_target_pairs={{0,8},{8,16},{16,24},{1,9},{9,17},{17,25},{2,10},{10,18},{18,26},{... | collective-permute-start | bytes 983048 | tf_op jit(solution)/shard_map/ppermute | solution.py:10
  40.9 1.2 %collective-permute-done.4 = bf16[2,2,160,256]{3,1,2,0:T(2,128)(2,1)S(1)} collective-permute-done((bf16[2,2,160,256]{3,1,2,0:T(2,128)(2,1)S(1)}, bf16[2,2,160,256]{3,1,2,0:T(2,128)(2,1)S(1)}, u32[]{:S(2)}, u32[]{:S(2)}) %collective-permute-start.4) | collective-permute-done | bytes 327712 | tf_op jit(solution)/shard_map/ppermute | solution.py:10
  42.2 1.1 %slice_maximum_fusion = (bf16[4,1,160,256]{3,1,2,0:T(2,128)(2,1)S(1)}, bf16[4,1,160,256]{3,1,2,0:T(2,128)(2,1)S(1)}) fusion(bf16[2,2,160,256]{3,1,2,0:T(2,128)(2,1)S(1)} %fusion.39, bf16[2,2,160,256]{3,1,2,0:T(2,128)(2,1)S(1)} %collective-permute-done.4), kind=kLoop, calls=%fused_computation.43 | loop fusion | flops 1310720 | bytes 1310720 | tf_op jit(solution)/shard_map/concatenate | solution.py:56
  43.3 0.1 copy.38
  43.4 1.5 %collective-permute-start.6 = (bf16[4,1,160,256]{3,2,1,0:T(8,128)(2,1)S(1)}, bf16[4,1,160,256]{3,2,1,0:T(8,128)(2,1)S(1)}, u32[]{:S(2)}, u32[]{:S(2)}) collective-permute-start(bf16[4,1,160,256]{3,2,1,0:T(8,128)(2,1)S(1)} %copy.38), channel_id=1, source_target_pairs={{1,0},{2,1},{3,2},{4,3},{5,4},{6,5},{7,6},{9,8},{10,9},{11,10},{12... | collective-permute-start | bytes 983048 | tf_op jit(solution)/shard_map/ppermute | solution.py:21
  44.8 0.1 copy.37
  44.9 5.0 %collective-permute-start.5 = (bf16[4,1,160,256]{3,2,1,0:T(8,128)(2,1)S(1)}, bf16[4,1,160,256]{3,2,1,0:T(8,128)(2,1)S(1)}, u32[]{:S(2)}, u32[]{:S(2)}) collective-permute-start(bf16[4,1,160,256]{3,2,1,0:T(8,128)(2,1)S(1)} %copy.37), channel_id=1, source_target_pairs={{0,1},{1,2},{2,3},{3,4},{4,5},{5,6},{6,7},{8,9},{9,10},{10,11},{11... | collective-permute-start | bytes 983048 | tf_op jit(solution)/shard_map/ppermute | solution.py:20
  49.9 2.9 %collective-permute-done.6 = bf16[4,1,160,256]{3,2,1,0:T(8,128)(2,1)S(1)} collective-permute-done((bf16[4,1,160,256]{3,2,1,0:T(8,128)(2,1)S(1)}, bf16[4,1,160,256]{3,2,1,0:T(8,128)(2,1)S(1)}, u32[]{:S(2)}, u32[]{:S(2)}) %collective-permute-start.6) | collective-permute-done | bytes 327712 | tf_op jit(solution)/shard_map/ppermute | solution.py:21
  52.8 0.5 copy.40
  53.3 9.9 %collective-permute-done.5 = bf16[4,1,160,256]{3,2,1,0:T(8,128)(2,1)S(1)} collective-permute-done((bf16[4,1,160,256]{3,2,1,0:T(8,128)(2,1)S(1)}, bf16[4,1,160,256]{3,2,1,0:T(8,128)(2,1)S(1)}, u32[]{:S(2)}, u32[]{:S(2)}) %collective-permute-start.5) | collective-permute-done | bytes 327712 | tf_op jit(solution)/shard_map/ppermute | solution.py:20
  63.2 0.5 copy.39
  63.7 2.3 %pad_maximum_fusion = bf16[4,4,160,256]{3,1,2,0:T(4,128)(2,1)S(1)} fusion(bf16[4,1,160,256]{3,1,2,0:T(2,128)(2,1)S(1)} %copy.40, bf16[2,2,160,256]{3,1,2,0:T(2,128)(2,1)S(1)} %fusion.39, bf16[2,2,160,256]{3,1,2,0:T(2,128)(2,1)S(1)} %collective-permute-done.4, bf16[4,1,160,256]{3,1,2,0:T(2,128)(2,1)S(1)} %copy.39), kind=kLoop, calls=%fused_computation.34 | loop fusion | flops 5242880 | bytes 2621440 | tf_op jit(solution)/shard_map/concatenate | solution.py:22
  66.1 1.0 %copy.41 = bf16[4,4,160,256]{3,0,2,1:T(4,128)(2,1)S(1)} copy(bf16[4,4,160,256]{3,1,2,0:T(4,128)(2,1)S(1)} %pad_maximum_fusion) | data formatting | bytes 2621440 | tf_op jit(solution)/shard_map/concatenate | solution.py:22
  67.1 2.2 %broadcast_in_dim.18 = bf16[4,4,2,160,256]{4,0,3,2,1:T(4,128)(2,1)} broadcast(bf16[4,4,160,256]{3,0,2,1:T(4,128)(2,1)S(1)} %copy.41), dimensions={0,1,3,4} | broadcast | bytes 3932160 | tf_op jit(solution)/shard_map/broadcast_in_dim | solution.py:57
  69.3 3.1 %broadcast_in_dim.19 = bf16[4,8,160,2,256]{4,0,3,2,1:T(4,128)(2,1)S(1)} broadcast(bf16[4,8,160,256]{3,0,2,1:T(4,128)(2,1)} %bitcast.55), dimensions={0,1,2,4} | broadcast | bytes 7864320 | tf_op jit(solution)/shard_map/broadcast_in_dim | solution.py:57
  72.4 1.4 %slice.29 = bf16[4,6,320,256]{3,0,2,1:T(4,128)(2,1)S(1)} slice(bf16[4,8,320,256]{3,0,2,1:T(4,128)(2,1)S(1)} %bitcast.52), slice={[0:4], [1:7], [0:320], [0:256]} | slice | bytes 7864320 | tf_op jit(solution)/shard_map/slice | solution.py:57
  73.8 1.7 %pad_bitcast_fusion = bf16[4,6,1,322,256]{4,0,3,1,2:T(4,128)(2,1)S(1)} fusion(bf16[4,6,320,256]{3,0,2,1:T(4,128)(2,1)S(1)} %slice.29), kind=kLoop, calls=%fused_computation.8 | loop fusion | bytes 7888896 | tf_op jit(solution)/shard_map/broadcast_in_dim | solution.py:29
  75.5 1.5 %pad.19 = bf16[4,6,1,328,256]{4,0,3,1,2:T(4,128)(2,1)S(1)} pad(bf16[4,6,1,322,256]{4,0,3,1,2:T(4,128)(2,1)S(1)} %pad_bitcast_fusion, bf16[]{:T(256)} %constant.7.clone.1), padding=0_0x0_0x0_0x0_6x0_0 | pad | bytes 7987202 | tf_op jit(solution)/shard_map/broadcast_in_dim | solution.py:29
  77.0 0.5 copy.43
  77.6 0.1 copy-done.2
  77.7 11.7 %fusion.23 = f32[2,4,8,41,256]{4,2,3,1,0:T(8,128)S(1)} fusion(bf16[3,3,3,256,256]{4,3,2,1,0:T(8,128)(2,1)S(1)} %copy-done, bf16[4,6,1,7,2,256]{5,3,4,1,0,2:T(8,128)(2,1)S(1)} %slice.30, bf16[4,6,1,8,41,256]{5,3,4,1,0,2:T(8,128)(2,1)S(1)} %copy.43, pred[8,41]{0,1:T(8,128)(4,1)S(1)} %copy-done.2), kind=kOutput, calls=%fused_computation.26 | convolution fusion | flops 9299542016 | bytes 10428744 | tf_op jit(solution)/shard_map/conv_general_dilated | solution.py:28
  89.4 1.0 %copy.44 = f32[2,4,8,41,256]{4,1,3,2,0:T(4,128)S(1)} copy(f32[2,4,8,41,256]{4,2,3,1,0:T(8,128)S(1)} %fusion.23) | data formatting | bytes 5373952 | tf_op jit(solution)/shard_map/conv_general_dilated | solution.py:28
  90.5 0.5 slice.31
  91.0 1.8 %multiply_convert_fusion = bf16[2,4,320,256]{3,2,1,0:T(8,128)(2,1)} fusion(f32[2,4,1,320,256]{4,1,3,0,2:T(4,128)S(1)} %slice.31), kind=kLoop, calls=%fused_computation.17 | loop fusion | flops 3276800 | bytes 3932160 | tf_op jit(solution)/shard_map/convert_element_type | solution.py:58
  (11 shorter events, 0.1 us)
Async XLA Ops:
  0.0 77.6 %copy-start = (bf16[3,3,3,256,256]{4,3,2,1,0:T(8,128)(2,1)S(1)}, bf16[3,3,3,256,256]{4,3,2,1,0:T(8,128)(2,1)}, u32[]{:S(2)}) copy-start(bf16[3,3,3,256,256]{4,3,2,1,0:T(8,128)(2,1)} %param.7) | copy-start | bytes 10616836
  0.0 7.8 %collective-permute-start = (bf16[2,2,160,16]{2,3,1,0:T(8,128)(2,1)}, bf16[2,2,160,16]{2,3,1,0:T(8,128)(2,1)}, u32[]{:S(2)}, u32[]{:S(2)}) collective-permute-start(bf16[2,2,160,16]{2,3,1,0:T(8,128)(2,1)} %param.4), channel_id=1, source_target_pairs={{0,16},{8,24},{1,17},{9,25},{2,18},{10,26},{3,19},{11,27},{4,20},{... | collective-permute-start | bytes 61448 | tf_op jit(solution)/shard_map/ppermute | solution.py:10
  5.7 2.8 %collective-permute-start.1 = (bf16[2,2,160,16]{2,3,1,0:T(8,128)(2,1)}, bf16[2,2,160,16]{2,3,1,0:T(8,128)(2,1)}, u32[]{:S(2)}, u32[]{:S(2)}) collective-permute-start(bf16[2,2,160,16]{2,3,1,0:T(8,128)(2,1)} %param.4), channel_id=1, source_target_pairs={{0,8},{8,16},{16,24},{1,9},{9,17},{17,25},{2,10},{10,18},{18,26},{... | collective-permute-start | bytes 61448 | tf_op jit(solution)/shard_map/ppermute | solution.py:10
  10.1 6.7 %collective-permute-start.3 = (bf16[6,2,160,16]{2,3,1,0:T(8,128)(2,1)S(1)}, bf16[6,2,160,16]{2,3,1,0:T(8,128)(2,1)S(1)}, u32[]{:S(2)}, u32[]{:S(2)}) collective-permute-start(bf16[6,2,160,16]{2,3,1,0:T(8,128)(2,1)S(1)} %constant_dynamic-update-slice_fusion), channel_id=1, source_target_pairs={{1,0},{2,1},{3,2},{4,3},{5,4},{6,5},{7,6},{9,8},{10,9},{11,10},{12... | collective-permute-start | bytes 184328 | tf_op jit(solution)/shard_map/ppermute | solution.py:21
  11.4 7.5 %collective-permute-start.2 = (bf16[6,2,160,16]{2,3,1,0:T(8,128)(2,1)S(1)}, bf16[6,2,160,16]{2,3,1,0:T(8,128)(2,1)S(1)}, u32[]{:S(2)}, u32[]{:S(2)}) collective-permute-start(bf16[6,2,160,16]{2,3,1,0:T(8,128)(2,1)S(1)} %constant_dynamic-update-slice_fusion), channel_id=1, source_target_pairs={{0,1},{1,2},{2,3},{3,4},{4,5},{5,6},{6,7},{8,9},{9,10},{10,11},{11... | collective-permute-start | bytes 184328 | tf_op jit(solution)/shard_map/ppermute | solution.py:20
  19.0 8.4 %copy-start.3 = (pred[8,21]{0,1:T(8,128)(4,1)S(1)}, pred[8,21]{0,1:T(8,128)(4,1)}, u32[]{:S(2)}) copy-start(pred[8,21]{0,1:T(8,128)(4,1)} %constant.41) | copy-start | bytes 508
  33.2 2.0 %copy-start.1 = (bf16[3,3,3,256,256]{4,3,2,1,0:T(8,128)(2,1)S(1)}, bf16[3,3,3,256,256]{4,3,2,1,0:T(8,128)(2,1)}, u32[]{:S(2)}) copy-start(bf16[3,3,3,256,256]{4,3,2,1,0:T(8,128)(2,1)} %param.6) | copy-start | bytes 10616836
  39.1 3.0 %collective-permute-start.4 = (bf16[2,2,160,256]{3,1,2,0:T(2,128)(2,1)S(1)}, bf16[2,2,160,256]{3,1,2,0:T(2,128)(2,1)S(1)}, u32[]{:S(2)}, u32[]{:S(2)}) collective-permute-start(bf16[2,2,160,256]{3,1,2,0:T(2,128)(2,1)S(1)} %fusion.39), channel_id=1, source_target_pairs={{0,8},{8,16},{16,24},{1,9},{9,17},{17,25},{2,10},{10,18},{18,26},{... | collective-permute-start | bytes 983048 | tf_op jit(solution)/shard_map/ppermute | solution.py:10
  43.4 9.4 %collective-permute-start.6 = (bf16[4,1,160,256]{3,2,1,0:T(8,128)(2,1)S(1)}, bf16[4,1,160,256]{3,2,1,0:T(8,128)(2,1)S(1)}, u32[]{:S(2)}, u32[]{:S(2)}) collective-permute-start(bf16[4,1,160,256]{3,2,1,0:T(8,128)(2,1)S(1)} %copy.38), channel_id=1, source_target_pairs={{1,0},{2,1},{3,2},{4,3},{5,4},{6,5},{7,6},{9,8},{10,9},{11,10},{12... | collective-permute-start | bytes 983048 | tf_op jit(solution)/shard_map/ppermute | solution.py:21
  44.9 18.3 %collective-permute-start.5 = (bf16[4,1,160,256]{3,2,1,0:T(8,128)(2,1)S(1)}, bf16[4,1,160,256]{3,2,1,0:T(8,128)(2,1)S(1)}, u32[]{:S(2)}, u32[]{:S(2)}) collective-permute-start(bf16[4,1,160,256]{3,2,1,0:T(8,128)(2,1)S(1)} %copy.37), channel_id=1, source_target_pairs={{0,1},{1,2},{2,3},{3,4},{4,5},{5,6},{6,7},{8,9},{9,10},{10,11},{11... | collective-permute-start | bytes 983048 | tf_op jit(solution)/shard_map/ppermute | solution.py:20
  77.0 0.7 copy-start.2
where the time goes:
time: 94.2 us; the launch traced here: 92.7 us
  local copies, waits for them, and re-layouts  28.8 us (31%)
  starting transfers between devices  21.9 us (23%)
  matrix products  18 us (19%)
  waiting for transfers between devices  16.9 us (18%)
  other arithmetic  6.8 us (7%)
    conv_general_dilated x3, matrix products, convolve(): lax.conv_general_dilated(padded[None], weight, (1, 1, 1), 'VALID', dimens...  18 us
    ppermute x2, waiting for transfers between devices, with_halo(): before = lax.ppermute(last, axis, up)  12 us
    conv_general_dilated x11, local copies, waits for them, and re-layouts, convolve(): lax.conv_general_dilated(padded[None], weight, (1, 1, 1), 'VALID', dimens...  11.3 us
    ppermute x3, starting transfers between devices, shifted(): return lax.ppermute(block, axis, route)  9.6 us
    ppermute x2, starting transfers between devices, with_halo(): before = lax.ppermute(last, axis, up)  9.58 us
    broadcast_in_dim x2, local copies, waits for them, and re-layouts, per_device(): enlarged = jnp.repeat(jnp.repeat(bordered, 2, axis=1), 2, axis=2)[:, 1:-1]  5.29 us
    broadcast_in_dim x5, local copies, waits for them, and re-layouts, convolve(): padded[None]  5.06 us
    ppermute x2, waiting for transfers between devices, with_halo(): after = lax.ppermute(first, axis, down)  3.74 us
  transfers between devices with their start and end apart: 7, of which 5 were waited for; matrix products, arithmetic and copies ran while one was open for 1% of the time, Pallas kernels for 0%

commit v1 on v0

v1 whole, which is shorter than its diff:
```python
import jax
import jax.numpy as jnp
from jax import lax
from jax.experimental import pallas as pl
from jax.experimental.pallas import tpu as pltpu
from jax.sharding import PartitionSpec as P

BF = jnp.bfloat16
F32 = jnp.float32
VM = pltpu.VMEM
SUB = 16

PAIRS = ((0, 2, -1), (1, 2, 1), (2, 1, -1), (1, 3, -1))


def swap(block, axis, distance):
    size = lax.axis_size(axis)
    return lax.ppermute(block, axis, [(i, i ^ distance) for i in range(size)])


def swap_across(block, axis):
    size = lax.axis_size(axis)
    pairs = []
    for i in range(size):
        k = (((i // 2) + 1) ^ 1) - 1
        if 0 <= k < size // 2:
            pairs.append((i, 2 * k + i % 2))
    return lax.ppermute(block, axis, pairs)


def silu(v):
    h = 0.5 * v
    return h + h * jnp.tanh(h)


def mm(a, b):
    return jnp.dot(a, b, preferred_element_type=F32)


def filtered(g0, g1, g2):
    s = 0.5 * (g0 + g2)
    h = 0.5 * g1
    return (g0, s + h, s - h, g2)


def summed(g0, g1, g2):
    return (-g0, (g0 + g1) + g2, g2)


def prepare_kernel(entry, mid, up, w_entry, w_mid, w_up):
    cin = entry.shape[0] // 27
    w_entry[...] = jnp.zeros_like(w_entry)
    for k in range(3):
        for a in range(3):
            for b in range(3):
                for c in range(3):
                    row = c * 256 + (a * 5 + b + k) * cin
                    at = (a * 9 + b * 3 + c) * cin
                    w_entry[k, row : row + cin, :] = entry[at : at + cin, :]
    ch = mid.shape[1]

    def step(i, carry):
        rows = pl.ds(pl.multiple_of(i * SUB, SUB), SUB)
        for c in range(3):
            g = [[mid[a * 9 + b * 3 + c, rows, :].astype(F32) for b in range(3)] for a in range(3)]
            t = [filtered(*[g[a][b] for a in range(3)]) for b in range(3)]
            to = pl.ds(pl.multiple_of(c * ch + i * SUB, SUB), SUB)
            for p in range(4):
                for q, value in enumerate(filtered(*[t[b][p] for b in range(3)])):
                    w_mid[p * 4 + q, to, :] = value.astype(BF)
        for a in range(3):
            g = [[up[a * 9 + b * 3 + c, rows, :].astype(F32) for c in range(3)] for b in range(3)]
            t = [summed(*[g[b][c] for b in range(3)]) for c in range(3)]
            to = pl.ds(pl.multiple_of(a * ch + i * SUB, SUB), SUB)
            for p in range(3):
                for q, value in enumerate(summed(*[t[c][p] for c in range(3)])):
                    w_up[p * 3 + q, to, :] = value.astype(BF)
        return carry

    lax.fori_loop(0, ch // SUB, step, 0)


def make_main(n_rows, cin, width, ch, n_x):
    k_tiles = width // SUB
    wide = width + 2 * SUB
    lanes = -(-width // 128) * 128

    def edged(y):
        s = lax.broadcasted_iota(jnp.int32, (SUB, ch), 0)
        before = pltpu.roll(y[width - SUB :], 1, 0)
        after = pltpu.roll(y[:SUB], SUB - 1, 0)
        before = jnp.where(s == 0, 0.0, before)
        after = jnp.where(s == SUB - 1, 0.0, after)
        return jnp.concatenate([before, y, after], axis=0).astype(BF)

    def three(v):
        return jnp.concatenate([v[c * SUB : c * SUB + width] for c in range(3)], axis=1)

    def kernel(where_ref, own, za, zb, w_entry, w_mid, w_up, out, lat, ent, bot, tmid, acc, sec, drow, prod, fin, done, sem):
        tm = where_ref[0]
        rw = where_ref[1]
        lat[...] = jnp.zeros_like(lat)
        z_odd = (rw // 2) % 2 == 1
        r_odd = rw % 2 == 1
        t_odd = tm % 2 == 1
        for bo in range(4):
            other_c = 1 - bo % 2
            if bo == 3:
                dx = 0
            elif bo == 2:
                dx = jnp.where(t_odd, 0, 1)
            elif bo == 1:
                dx = 1
            else:
                dx = jnp.where(t_odd, 1, min(2, n_x - 1))
            t_ok = tm - 3 + bo >= 0
            for ro in range(-2, 3):
                row_ok = jnp.logical_and(rw + ro >= 0, rw + ro < n_rows)
                ok = jnp.logical_and(t_ok, row_ok)
                y = ro % 2
                use_a = z_odd if ro < 0 else jnp.logical_not(z_odd)
                if ro == 0:
                    stays = None
                elif ro == -1:
                    stays = r_odd
                elif ro == 1:
                    stays = jnp.logical_not(r_odd)
                else:
                    stays = False
                for f in range(2):
                    for row in ((1,) if ro == -2 else (0,) if ro == 2 else (0, 1)):
                        h = 2 * (ro + 2) + row - 1
                        at = (y, dx, other_c, f, row)
                        if ro == 0:
                            v = own[at]
                        else:
                            v = jnp.where(use_a, za[at], zb[at])
                            if stays is not False:
                                v = jnp.where(stays, own[at], v)
                        lat[2 * bo + f, h * cin : (h + 1) * cin, :width] = jnp.where(ok, v, jnp.zeros_like(v))
        p = lax.broadcasted_iota(jnp.int32, (wide, lanes), 0)
        j = lax.broadcasted_iota(jnp.int32, (wide, lanes), 1)
        hit = jnp.logical_and(j == (p % SUB) * k_tiles + p // SUB - 1, j < width)
        order = jnp.where(hit, 1.0, 0.0).astype(BF)
        pad = jnp.zeros((ch - 15 * cin, lanes), BF)
        for f in range(6):
            for u in range(2):
                rows = [lat[f + a, 3 * u * cin : (3 * u + 5) * cin, :] for a in range(3)]
                stack = jnp.concatenate(rows + [pad], axis=0)
                patch = lax.dot_general(order, stack, (((1,), (1,)), ((), ())), preferred_element_type=F32)
                ent[f, u] = patch.astype(BF)
        for k in range(3):
            for u in range(2):
                r = 3 * u + k
                left = jnp.concatenate([three(ent[f, u]) for f in range(6)], axis=0)
                y = mm(left, w_entry[k])
                line = 2 * rw - 2 + r
                keep = jnp.where(jnp.logical_and(line >= 0, line < 2 * n_rows), 1.0, 0.0)
                y = y * keep
                for f in range(6):
                    bot[f, r] = edged(y[f * width : (f + 1) * width])
        for t in range(2):
            for k, (i0, i1, sign) in enumerate(PAIRS):
                for r in range(6):
                    v0, v1 = bot[2 * t + i0, r], bot[2 * t + i1, r]
                    tmid[k, t, r] = v0 + v1 if sign > 0 else v0 - v1
        for k in range(4):
            m = [prod.at[k % 2, q] for q in range(4)]
            for q, (i0, i1, sign) in enumerate(PAIRS):
                left = []
                for t in range(2):
                    for u in range(2):
                        v0, v1 = tmid[k, t, 2 * u + i0], tmid[k, t, 2 * u + i1]
                        left.append(three(v0 + v1 if sign > 0 else v0 - v1))
                m[q][...] = mm(jnp.concatenate(left, axis=0), w_mid[k * 4 + q])
            for q in range(2):
                value = (m[0][...] + m[1][...]) + m[2][...] if q == 0 else (m[1][...] - m[2][...]) - m[3][...]
                if k == 0:
                    acc[0, q] = value
                elif k == 1:
                    acc[0, q] = acc[0, q] + value
                    acc[1, q] = value
                elif k == 2:
                    acc[0, q] = acc[0, q] + value
                    acc[1, q] = acc[1, q] - value
                else:
                    acc[1, q] = acc[1, q] - value
        for t in range(2):
            for u in range(2):
                at = (2 * t + u) * width
                for dt in range(2):
                    for dr in range(2):
                        s, v = 2 * t + dt, 2 * u + dr
                        b = bot[s + 2, v + 1, SUB : SUB + width, :].astype(F32)
                        y = b + silu(acc[dt, dr, at : at + width, :])
                        line = 2 * rw - 1 + v
                        keep = jnp.where(jnp.logical_and(line >= 0, line < 2 * n_rows), 1.0, 0.0)
                        sec[s, v] = edged(y * keep)
        for s in range(4):
            for m in range(3):
                drow[s, m] = sec[s, m + 1] - sec[s, m]
        copies = []
        for t in range(2):
            for i in range(2):
                rows = (
                    [drow[t + a, i] for a in range(3)],
                    [sec[t + a, i + 1] for a in range(3)],
                    [drow[t + a, i + 1] for a in range(3)],
                )
                q = []
                for al in range(3):
                    diff = [x[SUB:] - x[:-SUB] for x in rows[al]]
                    mid_x = [x[SUB : SUB + width] for x in rows[al]]
                    m = [prod.at[(t * 2 + i) % 2, al, be * width : (be + 1) * width] for be in range(3)]
                    m[0][...] = mm(jnp.concatenate([d[:width] for d in diff], axis=1), w_up[al * 3])
                    m[1][...] = mm(jnp.concatenate(mid_x, axis=1), w_up[al * 3 + 1])
                    m[2][...] = mm(jnp.concatenate([d[SUB:] for d in diff], axis=1), w_up[al * 3 + 2])
                    q.append(m)
                for pr in range(2):
                    n = (t * 2 + i) * 2 + pr
                    for pc in range(2):
                        y = silu((q[1][1][...] + q[1][2 * pc][...]) + (q[2 * pr][1][...] + q[2 * pr][2 * pc][...]))
                        for kk in range(k_tiles):
                            for half in range(ch // 128):
                                part = slice(half * 128, half * 128 + 128)
                                fin[n % 2, half, pl.ds(2 * kk + pc, SUB, stride=2 * k_tiles), :] = y[kk * SUB : (kk + 1) * SUB, part]
                    even = jnp.concatenate([fin[n % 2, half] for half in range(ch // 128)], axis=1)
                    done[n] = even.astype(BF)
                    copy = pltpu.make_async_copy(done.at[n], out.at[t, 2 * i + pr], sem.at[n])
                    copy.start()
                    copies.append(copy)
        for copy in copies:
            copy.wait()

    return kernel


def per_device(latent, entry_kernel, middle_kernel, upper_kernel):
    n_tm, n_rows = lax.axis_size("tm"), lax.axis_size("rows")
    frames, height, width, cin = latent.shape
    ch = middle_kernel.shape[-1]
    wide = width + 2 * SUB
    vmem = pl.BlockSpec(memory_space=VM)
    w_entry, w_mid, w_up = pl.pallas_call(
        prepare_kernel,
        out_shape=(
            jax.ShapeDtypeStruct((3, 3 * 256, ch), BF),
            jax.ShapeDtypeStruct((16, 3 * ch, ch), BF),
            jax.ShapeDtypeStruct((9, 3 * ch, ch), BF),
        ),
        in_specs=[vmem] * 3,
        out_specs=(vmem,) * 3,
        compiler_params=pltpu.CompilerParams(vmem_limit_bytes=24 * 2**20),
        name="prepare",
    )(
        entry_kernel.reshape(27 * cin, ch),
        middle_kernel.reshape(27, ch, ch),
        upper_kernel.reshape(27, ch, ch),
    )
    x = jnp.transpose(latent, (0, 1, 3, 2))
    x = jnp.stack([x, swap(x, "tm", 1)])
    steps = [d for d in (2, 4) if d < n_tm]
    x = jnp.stack([x] + [lax.ppermute(x, "tm", [(i, (i + d) % n_tm) for i in range(n_tm)]) for d in steps])
    x = jnp.stack([x, swap(x, "rows", 1)])
    za, zb = swap(x, "rows", 2), swap_across(x, "rows")
    where = jnp.stack([lax.axis_index("tm"), lax.axis_index("rows")]).astype(jnp.int32)
    kernel = make_main(n_rows, cin, width, ch, 1 + len(steps))
    return pl.pallas_call(
        kernel,
        out_shape=jax.ShapeDtypeStruct((frames, 2 * height, 2 * width, ch), BF),
        in_specs=[pl.BlockSpec(memory_space=pltpu.SMEM)] + [vmem] * 6,
        out_specs=pl.BlockSpec(memory_space=pl.ANY),
        scratch_shapes=[
            VM((8, 8 * cin, -(-width // 128) * 128), BF),
            VM((6, 2, wide, ch), BF),
            VM((6, 6, wide, ch), BF),
            VM((4, 2, 6, wide, ch), BF),
            VM((2, 2, 4 * width, ch), F32),
            VM((4, 4, wide, ch), BF),
            VM((4, 3, wide, ch), BF),
            VM((2, 4, 4 * width, ch), F32),
            VM((2, ch // 128, 2 * width, 128), F32),
            VM((8, 2 * width, ch), BF),
            pltpu.SemaphoreType.DMA((8,)),
        ],
        compiler_params=pltpu.CompilerParams(vmem_limit_bytes=36 * 2**20),
        name="section",
    )(where, x, za, zb, w_entry, w_mid, w_up)


def solution(mesh):
    return jax.shard_map(
        per_device,
        mesh=mesh,
        in_specs=(P("tm", "rows", None, None), P(), P(), P()),
        out_specs=P("tm", "rows", None, None),
        check_vma=False,
    )
```

time: 94.2 us -> 37.6 us (0.40); the launches traced: 92.7 us -> 37.3 us
  local copies, waits for them, and re-layouts: 28.8 us -> 4.94 us
  matrix products: 18 us -> 0 us
  Pallas kernels: 0 us -> 14 us
  starting transfers between devices: 21.9 us -> 10.8 us
  waiting for transfers between devices: 16.9 us -> 6.61 us
  other arithmetic: 6.8 us -> 0.93 us
    conv_general_dilated x3 -> x0, matrix products: 18 us -> none  [convolve(): lax.conv_general_dilated(padded[None], weight, (1, 1, 1), 'VALID', dimens...]
    pallas_call x0 -> x2, Pallas kernels: none -> 14 us  [the longest x1 11.8 us: per_device(): pl.pallas_call(kernel, out_shape=jax.ShapeDtypeStruct((frames, 2 * height...]
    conv_general_dilated x11 -> x0, local copies, waits for them, and re-layouts: 11.3 us -> none  [convolve(): lax.conv_general_dilated(padded[None], weight, (1, 1, 1), 'VALID', dimens...]
    ppermute x7 -> x5, starting transfers between devices: 21.9 us -> 10.8 us  [the longest x3 7.22 us: swap(): return lax.ppermute(block, axis, [(i, i ^ distance) for i in range(size)])]
    broadcast_in_dim x7 -> x0, local copies, waits for them, and re-layouts: 10.3 us -> none  [the longest x2 5.29 us: per_device(): enlarged = jnp.repeat(jnp.repeat(bordered, 2, axis=1), 2, axis=2)[:, 1:-1]]
    ppermute x7 -> x5, waiting for transfers between devices: 16.9 us -> 6.61 us  [the longest x3 4.18 us: swap(): return lax.ppermute(block, axis, [(i, i ^ distance) for i in range(size)])]
    concatenate x2 -> x0, other arithmetic: 3.47 us -> none  [the longest x1 2.34 us: with_halo(): array = jnp.concatenate([before, array, after], axis=dim)]
    convert_element_type x4 -> x0, other arithmetic: 3.16 us -> none  [the longest x1 1.78 us: per_device(): return jax.nn.silu(convolve(enlarged, upper_kernel)).astype(jnp.bfloat16)]
  transfers between devices with their start and end apart: 7 -> 5, of which waited for: 5 -> 3; matrix products, arithmetic and copies ran while one was open for 1% -> 0% of each run, Pallas kernels for 0% -> 6%
where the time goes in v1:
time: 37.6 us; the launch traced here: 37.3 us
  Pallas kernels  14 us (37%)
  starting transfers between devices  10.8 us (29%)
  waiting for transfers between devices  6.61 us (18%)
  local copies, waits for them, and re-layouts  4.94 us (13%)
  other arithmetic  0.93 us (2%)
    pallas_call x1, Pallas kernels, per_device(): pl.pallas_call(kernel, out_shape=jax.ShapeDtypeStruct((frames, 2 * height...  11.8 us
    ppermute x3, starting transfers between devices, swap(): return lax.ppermute(block, axis, [(i, i ^ distance) for i in range(size)])  7.22 us
    unnamed x6, local copies, waits for them, and re-layouts  4.94 us
    ppermute x3, waiting for transfers between devices, swap(): return lax.ppermute(block, axis, [(i, i ^ distance) for i in range(size)])  4.18 us
    ppermute x1, starting transfers between devices, per_device(): lax.ppermute(x, 'tm', [(i, (i + d) % n_tm) for i in range(n_tm)])  2.89 us
    ppermute x1, waiting for transfers between devices, per_device(): lax.ppermute(x, 'tm', [(i, (i + d) % n_tm) for i in range(n_tm)])  2.42 us
    pallas_call x1, Pallas kernels, per_device(): pl.pallas_call(prepare_kernel, out_shape=(jax.ShapeDtypeStruct((3, 3 * 25...  2.21 us
    another operation x1, other arithmetic, per_device(): jnp.stack([x] + [lax.ppermute(x, 'tm', [(i, (i + d) % n_tm) for i in rang...  0.77 us
  transfers between devices with their start and end apart: 5, of which 3 were waited for; matrix products, arithmetic and copies ran while one was open for 0% of the time, Pallas kernels for 6%

profile of v1, /device:TPU:0, one launch (start us, length us, event | category | flops | bytes accessed | tf_op | source)
XLA Modules:
  0.0 37.3 jit_solution(9389819539518189750)
XLA Ops:
  0.0 0.5 %collective-permute-start = (bf16[2,2,16,160]{3,2,1,0:T(8,128)(2,1)}, bf16[2,2,16,160]{3,2,1,0:T(8,128)(2,1)S(1)}, u32[]{:S(2)}, u32[]{:S(2)}) collective-permute-start(bf16[2,2,16,160]{3,2,1,0:T(8,128)(2,1)} %bitcast.20), channel_id=1, source_target_pairs={{0,8},{8,0},{16,24},{24,16},{1,9},{9,1},{17,25},{25,17},{2,10},{10... | collective-permute-start | bytes 61448 | tf_op jit(solution)/shard_map/ppermute | solution.py:18
  0.5 1.1 %collective-permute-done = bf16[2,2,16,160]{3,2,1,0:T(8,128)(2,1)S(1)} collective-permute-done((bf16[2,2,16,160]{3,2,1,0:T(8,128)(2,1)}, bf16[2,2,16,160]{3,2,1,0:T(8,128)(2,1)S(1)}, u32[]{:S(2)}, u32[]{:S(2)}) %collective-permute-start) | collective-permute-done | bytes 20512 | tf_op jit(solution)/shard_map/ppermute | solution.py:18
  1.6 0.8 %fusion = (bf16[1,2,2,2,16,160]{5,4,3,2,1,0:T(8,128)(2,1)S(1)}, bf16[2,2,2,16,160]{4,3,2,1,0:T(8,128)(2,1)S(1)}) fusion(bf16[1,2,2,16,160]{4,3,2,1,0:T(8,128)(2,1)S(1)} %bitcast.22, bf16[1,2,2,16,160]{4,3,2,1,0:T(8,128)(2,1)} %bitcast.21), kind=kLoop, calls=%fused_computation.4 | loop fusion | flops 20480 | bytes 122880 | tf_op jit(solution)/shard_map/stack | solution.py:263
  2.3 2.9 %collective-permute-start.1 = (bf16[2,2,2,16,160]{4,3,2,1,0:T(8,128)(2,1)S(1)}, bf16[2,2,2,16,160]{4,3,2,1,0:T(8,128)(2,1)S(1)}, u32[]{:S(2)}, u32[]{:S(2)}) collective-permute-start(bf16[2,2,2,16,160]{4,3,2,1,0:T(8,128)(2,1)S(1)} %get-tuple-element.14), channel_id=1, source_target_pairs={{0,16},{8,24},{16,0},{24,8},{1,17},{9,25},{17,1},{25,9},{2,18},{10... | collective-permute-start | bytes 122888 | tf_op jit(solution)/shard_map/ppermute | solution.py:263
  5.2 2.4 %collective-permute-done.1 = bf16[2,2,2,16,160]{4,3,2,1,0:T(8,128)(2,1)S(1)} collective-permute-done((bf16[2,2,2,16,160]{4,3,2,1,0:T(8,128)(2,1)S(1)}, bf16[2,2,2,16,160]{4,3,2,1,0:T(8,128)(2,1)S(1)}, u32[]{:S(2)}, u32[]{:S(2)}) %collective-permute-start.1) | collective-permute-done | bytes 40992 | tf_op jit(solution)/shard_map/ppermute | solution.py:263
  7.7 1.9 %collective-permute-start.2 = (bf16[2,2,2,2,16,160]{5,4,3,2,1,0:T(8,128)(2,1)S(1)}, bf16[2,2,2,2,16,160]{5,4,3,2,1,0:T(8,128)(2,1)S(1)}, u32[]{:S(2)}, u32[]{:S(2)}) collective-permute-start(bf16[2,2,2,2,16,160]{5,4,3,2,1,0:T(8,128)(2,1)S(1)} %get-tuple-element.12), channel_id=1, source_target_pairs={{0,1},{1,0},{2,3},{3,2},{4,5},{5,4},{6,7},{7,6},{8,9},{9,8},{10,11... | collective-permute-start | bytes 245768 | tf_op jit(solution)/shard_map/ppermute | solution.py:18
  9.6 3.1 %collective-permute-done.2 = bf16[2,2,2,2,16,160]{5,4,3,2,1,0:T(8,128)(2,1)S(1)} collective-permute-done((bf16[2,2,2,2,16,160]{5,4,3,2,1,0:T(8,128)(2,1)S(1)}, bf16[2,2,2,2,16,160]{5,4,3,2,1,0:T(8,128)(2,1)S(1)}, u32[]{:S(2)}, u32[]{:S(2)}) %collective-permute-start.2) | collective-permute-done | bytes 81952 | tf_op jit(solution)/shard_map/ppermute | solution.py:18
  12.8 0.7 %collective-permute-start.4 = (bf16[2,2,2,2,2,16,160]{6,5,4,3,2,1,0:T(8,128)(2,1)S(1)}, bf16[2,2,2,2,2,16,160]{6,5,4,3,2,1,0:T(8,128)(2,1)S(1)}, u32[]{:S(2)}, u32[]{:S(2)}) collective-permute-start(bf16[2,2,2,2,2,16,160]{6,5,4,3,2,1,0:T(8,128)(2,1)S(1)} %pad_maximum_fusion.own), channel_id=1, source_target_pairs={{2,4},{3,5},{4,2},{5,3},{10,12},{11,13},{12,10},{13,11},{18,20},{1... | collective-permute-start | bytes 491528 | tf_op jit(solution)/shard_map/ppermute | solution.py:28
  13.5 4.8 %collective-permute-start.3 = (bf16[2,2,2,2,2,16,160]{6,5,4,3,2,1,0:T(8,128)(2,1)S(1)}, bf16[2,2,2,2,2,16,160]{6,5,4,3,2,1,0:T(8,128)(2,1)S(1)}, u32[]{:S(2)}, u32[]{:S(2)}) collective-permute-start(bf16[2,2,2,2,2,16,160]{6,5,4,3,2,1,0:T(8,128)(2,1)S(1)} %pad_maximum_fusion.own), channel_id=1, source_target_pairs={{0,2},{1,3},{2,0},{3,1},{4,6},{5,7},{6,4},{7,5},{8,10},{9,11},{10,... | collective-permute-start | bytes 491528 | tf_op jit(solution)/shard_map/ppermute | solution.py:18
  18.3 0.0 copy-start
  18.3 2.0 %copy-done = bf16[3,3,3,256,256]{4,3,2,1,0:T(8,128)(2,1)S(1)} copy-done((bf16[3,3,3,256,256]{4,3,2,1,0:T(8,128)(2,1)S(1)}, bf16[3,3,3,256,256]{4,3,2,1,0:T(8,128)(2,1)}, u32[]{:S(2)}) %copy-start) | copy-done | bytes 3538968
  20.3 0.0 copy-start.1
  20.3 2.0 %copy-done.1 = bf16[3,3,3,256,256]{4,3,2,1,0:T(8,128)(2,1)S(1)} copy-done((bf16[3,3,3,256,256]{4,3,2,1,0:T(8,128)(2,1)S(1)}, bf16[3,3,3,256,256]{4,3,2,1,0:T(8,128)(2,1)}, u32[]{:S(2)}) %copy-start.1) | copy-done | bytes 3538968
  22.3 0.0 copy-start.2
  22.3 0.9 %copy-done.2 = bf16[3,3,3,16,256]{4,3,2,1,0:T(8,128)(2,1)S(1)} copy-done((bf16[3,3,3,16,256]{4,3,2,1,0:T(8,128)(2,1)S(1)}, bf16[3,3,3,16,256]{4,3,2,1,0:T(8,128)(2,1)}, u32[]{:S(2)}) %copy-start.2) | copy-done | bytes 221208
  23.2 2.2 %prepare.1 = (bf16[3,768,256]{2,1,0:T(8,128)(2,1)S(1)}, bf16[16,768,256]{2,1,0:T(8,128)(2,1)S(1)}, bf16[9,768,256]{2,1,0:T(8,128)(2,1)S(1)}) custom-call(bf16[432,256]{1,0:T(8,128)(2,1)S(1)} %bitcast.17, bf16[27,256,256]{2,1,0:T(8,128)(2,1)S(1)} %bitcast.15, bf16[27,256,256]{2,1,0:T(8,128)(2,1)S(1)} %bitcast.16), custom_call_target="tpu_custom_call" | custom-call | tf_op jit(solution)/shard_map/prepare/pallas_call | solution.py:244
  25.4 0.1 pad_add_fusion.where_ref
  25.5 0.0 collective-permute-done.4.zb
  25.5 0.0 collective-permute-done.3.za
  25.5 11.8 %section.1 = bf16[2,4,320,256]{3,2,1,0:T(8,128)(2,1)} custom-call(s32[2]{0:T(128)S(1)} %pad_add_fusion.where_ref, bf16[2,2,2,2,2,16,160]{6,5,4,3,2,1,0:T(8,128)(2,1)S(1)} %pad_maximum_fusion.own, bf16[2,2,2,2,2,16,160]{6,5,4,3,2,1,0:T(8,128)(2,1)S(1)} %collective-permute-done.3.za, bf16[2,2,2,2,2,16,160]{6,5,4,3,2,1,0:T(8,128)(2,1)S(1)} %collective-permute-done.4.zb, ...), custom_call_target="tpu_custom_call" | custom-call | tf_op jit(solution)/shard_map/section/pallas_call | solution.py:268
  (2 shorter events, 0.1 us)
Async XLA Ops:
  0.0 1.6 %collective-permute-start = (bf16[2,2,16,160]{3,2,1,0:T(8,128)(2,1)}, bf16[2,2,16,160]{3,2,1,0:T(8,128)(2,1)S(1)}, u32[]{:S(2)}, u32[]{:S(2)}) collective-permute-start(bf16[2,2,16,160]{3,2,1,0:T(8,128)(2,1)} %bitcast.20), channel_id=1, source_target_pairs={{0,8},{8,0},{16,24},{24,16},{1,9},{9,1},{17,25},{25,17},{2,10},{10... | collective-permute-start | bytes 61448 | tf_op jit(solution)/shard_map/ppermute | solution.py:18
  2.3 5.3 %collective-permute-start.1 = (bf16[2,2,2,16,160]{4,3,2,1,0:T(8,128)(2,1)S(1)}, bf16[2,2,2,16,160]{4,3,2,1,0:T(8,128)(2,1)S(1)}, u32[]{:S(2)}, u32[]{:S(2)}) collective-permute-start(bf16[2,2,2,16,160]{4,3,2,1,0:T(8,128)(2,1)S(1)} %get-tuple-element.14), channel_id=1, source_target_pairs={{0,16},{8,24},{16,0},{24,8},{1,17},{9,25},{17,1},{25,9},{2,18},{10... | collective-permute-start | bytes 122888 | tf_op jit(solution)/shard_map/ppermute | solution.py:263
  7.7 5.1 %collective-permute-start.2 = (bf16[2,2,2,2,16,160]{5,4,3,2,1,0:T(8,128)(2,1)S(1)}, bf16[2,2,2,2,16,160]{5,4,3,2,1,0:T(8,128)(2,1)S(1)}, u32[]{:S(2)}, u32[]{:S(2)}) collective-permute-start(bf16[2,2,2,2,16,160]{5,4,3,2,1,0:T(8,128)(2,1)S(1)} %get-tuple-element.12), channel_id=1, source_target_pairs={{0,1},{1,0},{2,3},{3,2},{4,5},{5,4},{6,7},{7,6},{8,9},{9,8},{10,11... | collective-permute-start | bytes 245768 | tf_op jit(solution)/shard_map/ppermute | solution.py:18
  12.8 12.7 %collective-permute-start.4 = (bf16[2,2,2,2,2,16,160]{6,5,4,3,2,1,0:T(8,128)(2,1)S(1)}, bf16[2,2,2,2,2,16,160]{6,5,4,3,2,1,0:T(8,128)(2,1)S(1)}, u32[]{:S(2)}, u32[]{:S(2)}) collective-permute-start(bf16[2,2,2,2,2,16,160]{6,5,4,3,2,1,0:T(8,128)(2,1)S(1)} %pad_maximum_fusion.own), channel_id=1, source_target_pairs={{2,4},{3,5},{4,2},{5,3},{10,12},{11,13},{12,10},{13,11},{18,20},{1... | collective-permute-start | bytes 491528 | tf_op jit(solution)/shard_map/ppermute | solution.py:28
  13.5 12.0 %collective-permute-start.3 = (bf16[2,2,2,2,2,16,160]{6,5,4,3,2,1,0:T(8,128)(2,1)S(1)}, bf16[2,2,2,2,2,16,160]{6,5,4,3,2,1,0:T(8,128)(2,1)S(1)}, u32[]{:S(2)}, u32[]{:S(2)}) collective-permute-start(bf16[2,2,2,2,2,16,160]{6,5,4,3,2,1,0:T(8,128)(2,1)S(1)} %pad_maximum_fusion.own), channel_id=1, source_target_pairs={{0,2},{1,3},{2,0},{3,1},{4,6},{5,7},{6,4},{7,5},{8,10},{9,11},{10,... | collective-permute-start | bytes 491528 | tf_op jit(solution)/shard_map/ppermute | solution.py:18
  18.3 2.0 %copy-start = (bf16[3,3,3,256,256]{4,3,2,1,0:T(8,128)(2,1)S(1)}, bf16[3,3,3,256,256]{4,3,2,1,0:T(8,128)(2,1)}, u32[]{:S(2)}) copy-start(bf16[3,3,3,256,256]{4,3,2,1,0:T(8,128)(2,1)} %param.6) | copy-start | bytes 10616836
  20.3 2.0 %copy-start.1 = (bf16[3,3,3,256,256]{4,3,2,1,0:T(8,128)(2,1)S(1)}, bf16[3,3,3,256,256]{4,3,2,1,0:T(8,128)(2,1)}, u32[]{:S(2)}) copy-start(bf16[3,3,3,256,256]{4,3,2,1,0:T(8,128)(2,1)} %param.7) | copy-start | bytes 10616836
  22.3 0.9 %copy-start.2 = (bf16[3,3,3,16,256]{4,3,2,1,0:T(8,128)(2,1)S(1)}, bf16[3,3,3,16,256]{4,3,2,1,0:T(8,128)(2,1)}, u32[]{:S(2)}) copy-start(bf16[3,3,3,16,256]{4,3,2,1,0:T(8,128)(2,1)} %param.5) | copy-start | bytes 663556

commit v2 on v1

--- a/solution.py
+++ b/solution.py
@@ -47,37 +47,72 @@
     return (-g0, (g0 + g1) + g2, g2)
 
 
-def prepare_kernel(entry, mid, up, w_entry, w_mid, w_up):
+CHUNKS = 4
+
+
+def fetch(raw, here, sems):
+    size = raw.shape[1] // CHUNKS
+    copies = []
+    for n in range(CHUNKS):
+        part = pl.ds(n * size, size)
+        copy = pltpu.make_async_copy(raw.at[:, part], here.at[:, part], sems.at[n])
+        copy.start()
+        copies.append(copy)
+    return copies
+
+
+def prepare_middle(entry, raw, w_entry, w_mid, mid, sems):
+    ch = raw.shape[1]
+    steps = ch // SUB // CHUNKS
+    copies = fetch(raw, mid, sems)
     cin = entry.shape[0] // 27
     w_entry[...] = jnp.zeros_like(w_entry)
     for k in range(3):
         for a in range(3):
             for b in range(3):
                 for c in range(3):
-                    row = c * 256 + (a * 5 + b + k) * cin
+                    row = c * ch + (a * 5 + b + k) * cin
                     at = (a * 9 + b * 3 + c) * cin
                     w_entry[k, row : row + cin, :] = entry[at : at + cin, :]
-    ch = mid.shape[1]
-
-    def step(i, carry):
-        rows = pl.ds(pl.multiple_of(i * SUB, SUB), SUB)
-        for c in range(3):
-            g = [[mid[a * 9 + b * 3 + c, rows, :].astype(F32) for b in range(3)] for a in range(3)]
-            t = [filtered(*[g[a][b] for a in range(3)]) for b in range(3)]
-            to = pl.ds(pl.multiple_of(c * ch + i * SUB, SUB), SUB)
-            for p in range(4):
-                for q, value in enumerate(filtered(*[t[b][p] for b in range(3)])):
-                    w_mid[p * 4 + q, to, :] = value.astype(BF)
-        for a in range(3):
-            g = [[up[a * 9 + b * 3 + c, rows, :].astype(F32) for c in range(3)] for b in range(3)]
-            t = [summed(*[g[b][c] for b in range(3)]) for c in range(3)]
-            to = pl.ds(pl.multiple_of(a * ch + i * SUB, SUB), SUB)
-            for p in range(3):
-                for q, value in enumerate(summed(*[t[c][p] for c in range(3)])):
-                    w_up[p * 3 + q, to, :] = value.astype(BF)
-        return carry
-
-    lax.fori_loop(0, ch // SUB, step, 0)
+    for n, copy in enumerate(copies):
+        copy.wait()
+
+        def step(i, carry):
+            at = pl.multiple_of((n * steps + i) * SUB, SUB)
+            for c in range(3):
+                g = [[mid[a * 9 + b * 3 + c, pl.ds(at, SUB), :].astype(F32) for b in range(3)] for a in range(3)]
+                t = [filtered(*[g[a][b] for a in range(3)]) for b in range(3)]
+                for p in range(4):
+                    for q, value in enumerate(filtered(*[t[b][p] for b in range(3)])):
+                        w_mid[p * 4 + q, pl.ds(c * ch + at, SUB), :] = value.astype(BF)
+            return carry
+
+        lax.fori_loop(0, steps, step, 0)
+
+
+def prepare_upper(raw, w_up, up, sems):
+    ch = raw.shape[1]
+    steps = ch // SUB // CHUNKS
+    for n, copy in enumerate(fetch(raw, up, sems)):
+        copy.wait()
+
+        def step(i, carry):
+            at = pl.multiple_of((n * steps + i) * SUB, SUB)
+            for a in range(3):
+                g = [[up[a * 9 + b * 3 + c, pl.ds(at, SUB), :].astype(F32) for c in range(3)] for b in range(3)]
+                t = [summed(*[g[b][c] for b in range(3)]) for c in range(3)]
+                for p in range(3):
+                    for q, value in enumerate(summed(*[t[c][p] for c in range(3)])):
+                        w_up[p * 3 + q, pl.ds(a * ch + at, SUB), :] = value.astype(BF)
+            return carry
+
+        lax.fori_loop(0, steps, step, 0)
+
+
+def pack(latent, packed):
+    blocks, _, _ = latent.shape
+    packed[:blocks] = latent[:, :, :128]
+    packed[blocks] = jnp.concatenate([latent[i, :, 128:] for i in range(blocks)], axis=1)
 
 
 def make_main(n_rows, cin, width, ch, n_x):
@@ -130,14 +165,21 @@
                 for f in range(2):
                     for row in ((1,) if ro == -2 else (0,) if ro == 2 else (0, 1)):
                         h = 2 * (ro + 2) + row - 1
-                        at = (y, dx, other_c, f, row)
-                        if ro == 0:
-                            v = own[at]
-                        else:
-                            v = jnp.where(use_a, za[at], zb[at])
-                            if stays is not False:
-                                v = jnp.where(stays, own[at], v)
-                        lat[2 * bo + f, h * cin : (h + 1) * cin, :width] = jnp.where(ok, v, jnp.zeros_like(v))
+                        n = 2 * f + row
+                        for tile in (n, 4):
+                            at = (y, dx, other_c, tile)
+                            if ro == 0:
+                                v = own[at]
+                            else:
+                                v = jnp.where(use_a, za[at], zb[at])
+                                if stays is not False:
+                                    v = jnp.where(stays, own[at], v)
+                            v = jnp.where(ok, v, jnp.zeros_like(v))
+                            if tile == n:
+                                lat[2 * bo + f, h * cin : (h + 1) * cin, :128] = v
+                            else:
+                                v = v[:, n * (width - 128) : (n + 1) * (width - 128)]
+                                lat[2 * bo + f, h * cin : (h + 1) * cin, 128:width] = v
         p = lax.broadcasted_iota(jnp.int32, (wide, lanes), 0)
         j = lax.broadcasted_iota(jnp.int32, (wide, lanes), 1)
         hit = jnp.logical_and(j == (p % SUB) * k_tiles + p // SUB - 1, j < width)
@@ -164,35 +206,32 @@
                 for r in range(6):
                     v0, v1 = bot[2 * t + i0, r], bot[2 * t + i1, r]
                     tmid[k, t, r] = v0 + v1 if sign > 0 else v0 - v1
-        for k in range(4):
-            m = [prod.at[k % 2, q] for q in range(4)]
-            for q, (i0, i1, sign) in enumerate(PAIRS):
-                left = []
-                for t in range(2):
+            for k in range(4):
+                m = [prod.at[k % 2, q, t] for q in range(4)]
+                for q, (i0, i1, sign) in enumerate(PAIRS):
+                    left = []
                     for u in range(2):
                         v0, v1 = tmid[k, t, 2 * u + i0], tmid[k, t, 2 * u + i1]
                         left.append(three(v0 + v1 if sign > 0 else v0 - v1))
-                m[q][...] = mm(jnp.concatenate(left, axis=0), w_mid[k * 4 + q])
-            for q in range(2):
-                value = (m[0][...] + m[1][...]) + m[2][...] if q == 0 else (m[1][...] - m[2][...]) - m[3][...]
-                if k == 0:
-                    acc[0, q] = value
-                elif k == 1:
-                    acc[0, q] = acc[0, q] + value
-                    acc[1, q] = value
-                elif k == 2:
-                    acc[0, q] = acc[0, q] + value
-                    acc[1, q] = acc[1, q] - value
-                else:
-                    acc[1, q] = acc[1, q] - value
-        for t in range(2):
+                    m[q][...] = mm(jnp.concatenate(left, axis=0), w_mid[k * 4 + q])
+                for q in range(2):
+                    value = (m[0][...] + m[1][...]) + m[2][...] if q == 0 else (m[1][...] - m[2][...]) - m[3][...]
+                    if k == 0:
+                        acc[t, 0, q] = value
+                    elif k == 1:
+                        acc[t, 0, q] = acc[t, 0, q] + value
+                        acc[t, 1, q] = value
+                    elif k == 2:
+                        acc[t, 0, q] = acc[t, 0, q] + value
+                        acc[t, 1, q] = acc[t, 1, q] - value
+                    else:
+                        acc[t, 1, q] = acc[t, 1, q] - value
             for u in range(2):
-                at = (2 * t + u) * width
                 for dt in range(2):
                     for dr in range(2):
                         s, v = 2 * t + dt, 2 * u + dr
                         b = bot[s + 2, v + 1, SUB : SUB + width, :].astype(F32)
-                        y = b + silu(acc[dt, dr, at : at + width, :])
+                        y = b + silu(acc[t, dt, dr, u * width : (u + 1) * width, :])
                         line = 2 * rw - 1 + v
                         keep = jnp.where(jnp.logical_and(line >= 0, line < 2 * n_rows), 1.0, 0.0)
                         sec[s, v] = edged(y * keep)
@@ -211,7 +250,7 @@
                 for al in range(3):
                     diff = [x[SUB:] - x[:-SUB] for x in rows[al]]
                     mid_x = [x[SUB : SUB + width] for x in rows[al]]
-                    m = [prod.at[(t * 2 + i) % 2, al, be * width : (be + 1) * width] for be in range(3)]
+                    m = [prod.at[i, al, be // 2, be % 2 * width : (be % 2 + 1) * width] for be in range(3)]
                     m[0][...] = mm(jnp.concatenate([d[:width] for d in diff], axis=1), w_up[al * 3])
                     m[1][...] = mm(jnp.concatenate(mid_x, axis=1), w_up[al * 3 + 1])
                     m[2][...] = mm(jnp.concatenate([d[SUB:] for d in diff], axis=1), w_up[al * 3 + 2])
@@ -241,28 +280,46 @@
     ch = middle_kernel.shape[-1]
     wide = width + 2 * SUB
     vmem = pl.BlockSpec(memory_space=VM)
-    w_entry, w_mid, w_up = pl.pallas_call(
-        prepare_kernel,
-        out_shape=(
-            jax.ShapeDtypeStruct((3, 3 * 256, ch), BF),
-            jax.ShapeDtypeStruct((16, 3 * ch, ch), BF),
-            jax.ShapeDtypeStruct((9, 3 * ch, ch), BF),
-        ),
-        in_specs=[vmem] * 3,
-        out_specs=(vmem,) * 3,
-        compiler_params=pltpu.CompilerParams(vmem_limit_bytes=24 * 2**20),
-        name="prepare",
-    )(
-        entry_kernel.reshape(27 * cin, ch),
-        middle_kernel.reshape(27, ch, ch),
-        upper_kernel.reshape(27, ch, ch),
-    )
-    x = jnp.transpose(latent, (0, 1, 3, 2))
-    x = jnp.stack([x, swap(x, "tm", 1)])
+    small = pltpu.CompilerParams(vmem_limit_bytes=6 * 2**20)
+    keep = lambda w: pltpu.with_memory_space_constraint(w, pltpu.HBM)
+    hbm = pl.BlockSpec(memory_space=pltpu.HBM)
+    fetched = [VM((27, ch, ch), BF), pltpu.SemaphoreType.DMA((CHUNKS,))]
+    w_entry, w_mid = pl.pallas_call(
+        prepare_middle,
+        out_shape=(VM((3, 3 * ch, ch), BF), VM((16, 3 * ch, ch), BF)),
+        in_specs=[vmem, hbm],
+        out_specs=(vmem, vmem),
+        scratch_shapes=fetched,
+        compiler_params=small,
+        name="prepare_middle",
+    )(entry_kernel.reshape(27 * cin, ch), keep(middle_kernel.reshape(27, ch, ch)))
+    w_up = pl.pallas_call(
+        prepare_upper,
+        out_shape=VM((9, 3 * ch, ch), BF),
+        in_specs=[hbm],
+        out_specs=vmem,
+        scratch_shapes=fetched,
+        compiler_params=small,
+        name="prepare_upper",
+    )(keep(upper_kernel.reshape(27, ch, ch)))
+    x = jnp.transpose(latent, (0, 1, 3, 2)).reshape(frames * height, cin, width)
+    x = pl.pallas_call(
+        pack,
+        out_shape=jax.ShapeDtypeStruct((frames * height + 1, cin, 128), BF),
+        in_specs=[vmem],
+        out_specs=vmem,
+        compiler_params=small,
+        name="pack",
+    )(x)
+    other = swap(x, "tm", 1)
+    x = jnp.stack([x, other])
     steps = [d for d in (2, 4) if d < n_tm]
-    x = jnp.stack([x] + [lax.ppermute(x, "tm", [(i, (i + d) % n_tm) for i in range(n_tm)]) for d in steps])
-    x = jnp.stack([x, swap(x, "rows", 1)])
-    za, zb = swap(x, "rows", 2), swap_across(x, "rows")
+    others = [lax.ppermute(x, "tm", [(i, (i + d) % n_tm) for i in range(n_tm)]) for d in steps]
+    x = jnp.stack([x] + others)
+    other = swap(x, "rows", 1)
+    x = jnp.stack([x, other])
+    za = swap(x, "rows", 2)
+    zb = swap_across(x, "rows")
     where = jnp.stack([lax.axis_index("tm"), lax.axis_index("rows")]).astype(jnp.int32)
     kernel = make_main(n_rows, cin, width, ch, 1 + len(steps))
     return pl.pallas_call(
@@ -275,15 +332,15 @@
             VM((6, 2, wide, ch), BF),
             VM((6, 6, wide, ch), BF),
             VM((4, 2, 6, wide, ch), BF),
-            VM((2, 2, 4 * width, ch), F32),
+            VM((2, 2, 2, 2 * width, ch), F32),
             VM((4, 4, wide, ch), BF),
             VM((4, 3, wide, ch), BF),
-            VM((2, 4, 4 * width, ch), F32),
+            VM((2, 4, 2, 2 * width, ch), F32),
             VM((2, ch // 128, 2 * width, 128), F32),
             VM((8, 2 * width, ch), BF),
             pltpu.SemaphoreType.DMA((8,)),
         ],
-        compiler_params=pltpu.CompilerParams(vmem_limit_bytes=36 * 2**20),
+        compiler_params=pltpu.CompilerParams(vmem_limit_bytes=32 * 2**20),
         name="section",
     )(where, x, za, zb, w_entry, w_mid, w_up)
 

time: 37.6 us -> 34 us (0.904)
  local copies, waits for them, and re-layouts: 4.94 us -> 0.76 us
  Pallas kernels: 14 us -> 16.5 us
  waiting for transfers between devices: 6.61 us -> 5.25 us
  other arithmetic: 0.93 us -> 0.12 us
    unnamed x6 -> x4, local copies, waits for them, and re-layouts: 4.94 us -> 0.76 us
    pallas_call x1 -> x3, Pallas kernels: 2.21 us -> 4.93 us  [the longest x1 2.6 us: per_device(): pl.pallas_call(prepare_middle, out_shape=(VM((3, 3 * ch, ch), BF), VM((16...]
    ppermute x3, waiting for transfers between devices: 4.18 us -> 3.27 us  [swap(): return lax.ppermute(block, axis, [(i, i ^ distance) for i in range(size)])]
    another operation x3, other arithmetic: 0.85 us -> 0.04 us  [the longest x2 0.03 us: per_device(): x = jnp.stack([x, other])]
    ppermute x1, waiting for transfers between devices: 2.42 us -> 1.98 us  [per_device(): lax.ppermute(x, 'tm', [(i, (i + d) % n_tm) for i in range(n_tm)])]
  transfers between devices with their start and end apart: 5 -> 5, of which waited for: 3 -> 3; matrix products, arithmetic and copies ran while one was open for 0% -> 0% of each run, Pallas kernels for 6% -> 14%
where the time goes in v2:
time: 34 us; the launch traced here: 33.8 us
  Pallas kernels  16.5 us (49%)
  starting transfers between devices  11.1 us (33%)
  waiting for transfers between devices  5.25 us (15%)
  local copies, waits for them, and re-layouts  0.76 us (2%)
    pallas_call x1, Pallas kernels, per_device(): pl.pallas_call(kernel, out_shape=jax.ShapeDtypeStruct((frames, 2 * height...  11.6 us
    ppermute x3, starting transfers between devices, swap(): return lax.ppermute(block, axis, [(i, i ^ distance) for i in range(size)])  7.57 us
    ppermute x3, waiting for transfers between devices, swap(): return lax.ppermute(block, axis, [(i, i ^ distance) for i in range(size)])  3.27 us
    ppermute x1, starting transfers between devices, per_device(): lax.ppermute(x, 'tm', [(i, (i + d) % n_tm) for i in range(n_tm)])  2.89 us
    pallas_call x1, Pallas kernels, per_device(): pl.pallas_call(prepare_middle, out_shape=(VM((3, 3 * ch, ch), BF), VM((16...  2.6 us
    pallas_call x1, Pallas kernels, per_device(): pl.pallas_call(prepare_upper, out_shape=VM((9, 3 * ch, ch), BF), in_specs...  2.26 us
    ppermute x1, waiting for transfers between devices, per_device(): lax.ppermute(x, 'tm', [(i, (i + d) % n_tm) for i in range(n_tm)])  1.98 us
    unnamed x4, local copies, waits for them, and re-layouts  0.76 us
  transfers between devices with their start and end apart: 5, of which 3 were waited for; matrix products, arithmetic and copies ran while one was open for 0% of the time, Pallas kernels for 14%

profile of v2, /device:TPU:0, one launch (start us, length us, event | category | flops | bytes accessed | tf_op | source)
XLA Modules:
  0.0 33.8 jit_solution(8199832401410550154)
XLA Ops:
  0.0 0.0 copy-start.1
  0.0 0.8 %copy-done.1 = bf16[2,2,160,16]{2,3,1,0:T(8,128)(2,1)S(1)} copy-done((bf16[2,2,160,16]{2,3,1,0:T(8,128)(2,1)S(1)}, bf16[2,2,160,16]{2,3,1,0:T(8,128)(2,1)}, u32[]{:S(2)}) %copy-start.1) | copy-done | bytes 20504
  0.8 0.1 pack.1
  0.8 0.5 %collective-permute-start = (bf16[5,16,128]{2,1,0:T(8,128)(2,1)S(1)}, bf16[5,16,128]{2,1,0:T(8,128)(2,1)S(1)}, u32[]{:S(2)}, u32[]{:S(2)}) collective-permute-start(bf16[5,16,128]{2,1,0:T(8,128)(2,1)S(1)} %pack.1), channel_id=1, source_target_pairs={{0,8},{8,0},{16,24},{24,16},{1,9},{9,1},{17,25},{25,17},{2,10},{10... | collective-permute-start | bytes 61448 | tf_op jit(solution)/shard_map/ppermute | solution.py:18
  1.3 0.8 %collective-permute-done = bf16[5,16,128]{2,1,0:T(8,128)(2,1)S(1)} collective-permute-done((bf16[5,16,128]{2,1,0:T(8,128)(2,1)S(1)}, bf16[5,16,128]{2,1,0:T(8,128)(2,1)S(1)}, u32[]{:S(2)}, u32[]{:S(2)}) %collective-permute-start) | collective-permute-done | bytes 20512 | tf_op jit(solution)/shard_map/ppermute | solution.py:18
  2.2 2.9 %collective-permute-start.1 = (bf16[2,5,16,128]{3,2,1,0:T(8,128)(2,1)S(1)}, bf16[2,5,16,128]{3,2,1,0:T(8,128)(2,1)S(1)}, u32[]{:S(2)}, u32[]{:S(2)}) collective-permute-start(bf16[2,5,16,128]{3,2,1,0:T(8,128)(2,1)S(1)} %get-tuple-element.12), channel_id=1, source_target_pairs={{0,16},{8,24},{16,0},{24,8},{1,17},{9,25},{17,1},{25,9},{2,18},{10... | collective-permute-start | bytes 122888 | tf_op jit(solution)/shard_map/ppermute | solution.py:317
  5.1 2.0 %collective-permute-done.1 = bf16[2,5,16,128]{3,2,1,0:T(8,128)(2,1)S(1)} collective-permute-done((bf16[2,5,16,128]{3,2,1,0:T(8,128)(2,1)S(1)}, bf16[2,5,16,128]{3,2,1,0:T(8,128)(2,1)S(1)}, u32[]{:S(2)}, u32[]{:S(2)}) %collective-permute-start.1) | collective-permute-done | bytes 40992 | tf_op jit(solution)/shard_map/ppermute | solution.py:317
  7.1 2.1 %collective-permute-start.2 = (bf16[2,2,5,16,128]{4,3,2,1,0:T(8,128)(2,1)S(1)}, bf16[2,2,5,16,128]{4,3,2,1,0:T(8,128)(2,1)S(1)}, u32[]{:S(2)}, u32[]{:S(2)}) collective-permute-start(bf16[2,2,5,16,128]{4,3,2,1,0:T(8,128)(2,1)S(1)} %get-tuple-element.10), channel_id=1, source_target_pairs={{0,1},{1,0},{2,3},{3,2},{4,5},{5,4},{6,7},{7,6},{8,9},{9,8},{10,11... | collective-permute-start | bytes 245768 | tf_op jit(solution)/shard_map/ppermute | solution.py:18
  9.2 2.4 %collective-permute-done.2 = bf16[2,2,5,16,128]{4,3,2,1,0:T(8,128)(2,1)S(1)} collective-permute-done((bf16[2,2,5,16,128]{4,3,2,1,0:T(8,128)(2,1)S(1)}, bf16[2,2,5,16,128]{4,3,2,1,0:T(8,128)(2,1)S(1)}, u32[]{:S(2)}, u32[]{:S(2)}) %collective-permute-start.2) | collective-permute-done | bytes 81952 | tf_op jit(solution)/shard_map/ppermute | solution.py:18
  11.6 0.7 %collective-permute-start.4 = (bf16[2,2,2,5,16,128]{5,4,3,2,1,0:T(8,128)(2,1)S(1)}, bf16[2,2,2,5,16,128]{5,4,3,2,1,0:T(8,128)(2,1)S(1)}, u32[]{:S(2)}, u32[]{:S(2)}) collective-permute-start(bf16[2,2,2,5,16,128]{5,4,3,2,1,0:T(8,128)(2,1)S(1)} %pad_maximum_fusion.own), channel_id=1, source_target_pairs={{2,4},{3,5},{4,2},{5,3},{10,12},{11,13},{12,10},{13,11},{18,20},{1... | collective-permute-start | bytes 491528 | tf_op jit(solution)/shard_map/ppermute | solution.py:28
  12.3 5.0 %collective-permute-start.3 = (bf16[2,2,2,5,16,128]{5,4,3,2,1,0:T(8,128)(2,1)S(1)}, bf16[2,2,2,5,16,128]{5,4,3,2,1,0:T(8,128)(2,1)S(1)}, u32[]{:S(2)}, u32[]{:S(2)}) collective-permute-start(bf16[2,2,2,5,16,128]{5,4,3,2,1,0:T(8,128)(2,1)S(1)} %pad_maximum_fusion.own), channel_id=1, source_target_pairs={{0,2},{1,3},{2,0},{3,1},{4,6},{5,7},{6,4},{7,5},{8,10},{9,11},{10,... | collective-permute-start | bytes 491528 | tf_op jit(solution)/shard_map/ppermute | solution.py:18
  17.3 0.0 copy-start
  17.3 2.3 %prepare_upper.1.w_up = bf16[9,768,256]{2,1,0:T(8,128)(2,1)S(1)} custom-call(bf16[27,256,256]{2,1,0:T(8,128)(2,1)} %bitcast.19), custom_call_target="tpu_custom_call" | custom-call | tf_op jit(solution)/shard_map/prepare_upper/pallas_call | solution.py:296
  19.5 0.0 copy-done
  19.5 2.6 %prepare_middle.1 = (bf16[3,768,256]{2,1,0:T(8,128)(2,1)S(1)}, bf16[16,768,256]{2,1,0:T(8,128)(2,1)S(1)}) custom-call(bf16[432,256]{1,0:T(8,128)(2,1)S(1)} %bitcast.16, bf16[27,256,256]{2,1,0:T(8,128)(2,1)} %bitcast.20), custom_call_target="tpu_custom_call" | custom-call | tf_op jit(solution)/shard_map/prepare_middle/pallas_call | solution.py:287
  22.1 0.1 pad_add_fusion.where_ref
  22.2 0.0 collective-permute-done.4.zb
  22.2 0.0 collective-permute-done.3.za
  22.2 11.6 %section.1 = bf16[2,4,320,256]{3,2,1,0:T(8,128)(2,1)} custom-call(s32[2]{0:T(128)S(1)} %pad_add_fusion.where_ref, bf16[2,2,2,5,16,128]{5,4,3,2,1,0:T(8,128)(2,1)S(1)} %pad_maximum_fusion.own, bf16[2,2,2,5,16,128]{5,4,3,2,1,0:T(8,128)(2,1)S(1)} %collective-permute-done.3.za, bf16[2,2,2,5,16,128]{5,4,3,2,1,0:T(8,128)(2,1)S(1)} %collective-permute-done.4.zb, ...), custom_call_target="tpu_custom_call" | custom-call | tf_op jit(solution)/shard_map/section/pallas_call | solution.py:325
  (3 shorter events, 0.0 us)
Async XLA Ops:
  0.0 0.8 %copy-start.1 = (bf16[2,2,160,16]{2,3,1,0:T(8,128)(2,1)S(1)}, bf16[2,2,160,16]{2,3,1,0:T(8,128)(2,1)}, u32[]{:S(2)}) copy-start(bf16[2,2,160,16]{2,3,1,0:T(8,128)(2,1)} %param.4) | copy-start | bytes 61444
  0.8 1.3 %collective-permute-start = (bf16[5,16,128]{2,1,0:T(8,128)(2,1)S(1)}, bf16[5,16,128]{2,1,0:T(8,128)(2,1)S(1)}, u32[]{:S(2)}, u32[]{:S(2)}) collective-permute-start(bf16[5,16,128]{2,1,0:T(8,128)(2,1)S(1)} %pack.1), channel_id=1, source_target_pairs={{0,8},{8,0},{16,24},{24,16},{1,9},{9,1},{17,25},{25,17},{2,10},{10... | collective-permute-start | bytes 61448 | tf_op jit(solution)/shard_map/ppermute | solution.py:18
  2.2 4.9 %collective-permute-start.1 = (bf16[2,5,16,128]{3,2,1,0:T(8,128)(2,1)S(1)}, bf16[2,5,16,128]{3,2,1,0:T(8,128)(2,1)S(1)}, u32[]{:S(2)}, u32[]{:S(2)}) collective-permute-start(bf16[2,5,16,128]{3,2,1,0:T(8,128)(2,1)S(1)} %get-tuple-element.12), channel_id=1, source_target_pairs={{0,16},{8,24},{16,0},{24,8},{1,17},{9,25},{17,1},{25,9},{2,18},{10... | collective-permute-start | bytes 122888 | tf_op jit(solution)/shard_map/ppermute | solution.py:317
  7.1 4.5 %collective-permute-start.2 = (bf16[2,2,5,16,128]{4,3,2,1,0:T(8,128)(2,1)S(1)}, bf16[2,2,5,16,128]{4,3,2,1,0:T(8,128)(2,1)S(1)}, u32[]{:S(2)}, u32[]{:S(2)}) collective-permute-start(bf16[2,2,5,16,128]{4,3,2,1,0:T(8,128)(2,1)S(1)} %get-tuple-element.10), channel_id=1, source_target_pairs={{0,1},{1,0},{2,3},{3,2},{4,5},{5,4},{6,7},{7,6},{8,9},{9,8},{10,11... | collective-permute-start | bytes 245768 | tf_op jit(solution)/shard_map/ppermute | solution.py:18
  11.6 10.6 %collective-permute-start.4 = (bf16[2,2,2,5,16,128]{5,4,3,2,1,0:T(8,128)(2,1)S(1)}, bf16[2,2,2,5,16,128]{5,4,3,2,1,0:T(8,128)(2,1)S(1)}, u32[]{:S(2)}, u32[]{:S(2)}) collective-permute-start(bf16[2,2,2,5,16,128]{5,4,3,2,1,0:T(8,128)(2,1)S(1)} %pad_maximum_fusion.own), channel_id=1, source_target_pairs={{2,4},{3,5},{4,2},{5,3},{10,12},{11,13},{12,10},{13,11},{18,20},{1... | collective-permute-start | bytes 491528 | tf_op jit(solution)/shard_map/ppermute | solution.py:28
  12.3 9.9 %collective-permute-start.3 = (bf16[2,2,2,5,16,128]{5,4,3,2,1,0:T(8,128)(2,1)S(1)}, bf16[2,2,2,5,16,128]{5,4,3,2,1,0:T(8,128)(2,1)S(1)}, u32[]{:S(2)}, u32[]{:S(2)}) collective-permute-start(bf16[2,2,2,5,16,128]{5,4,3,2,1,0:T(8,128)(2,1)S(1)} %pad_maximum_fusion.own), channel_id=1, source_target_pairs={{0,2},{1,3},{2,0},{3,1},{4,6},{5,7},{6,4},{7,5},{8,10},{9,11},{10,... | collective-permute-start | bytes 491528 | tf_op jit(solution)/shard_map/ppermute | solution.py:18
  17.3 2.3 %copy-start = (bf16[3,3,3,16,256]{4,3,2,1,0:T(8,128)(2,1)S(1)}, bf16[3,3,3,16,256]{4,3,2,1,0:T(8,128)(2,1)}, u32[]{:S(2)}) copy-start(bf16[3,3,3,16,256]{4,3,2,1,0:T(8,128)(2,1)} %param.5) | copy-start | bytes 663556

commit v3 on v2

--- a/solution.py
+++ b/solution.py
@@ -61,12 +61,15 @@
     return copies
 
 
-def prepare_middle(entry, raw, w_entry, w_mid, mid, sems):
+def prepare_middle(first, raw, w_entry, w_mid, mid, sems, entry, sem):
+    taken = pltpu.make_async_copy(first, entry, sem)
+    taken.start()
     ch = raw.shape[1]
     steps = ch // SUB // CHUNKS
     copies = fetch(raw, mid, sems)
     cin = entry.shape[0] // 27
     w_entry[...] = jnp.zeros_like(w_entry)
+    taken.wait()
     for k in range(3):
         for a in range(3):
             for b in range(3):
@@ -131,7 +134,7 @@
     def three(v):
         return jnp.concatenate([v[c * SUB : c * SUB + width] for c in range(3)], axis=1)
 
-    def kernel(where_ref, own, za, zb, w_entry, w_mid, w_up, out, lat, ent, bot, tmid, acc, sec, drow, prod, fin, done, sem):
+    def kernel(where_ref, own0, own1, za0, za1, zb0, zb1, w_entry, w_mid, w_up, out, lat, ent, bot, tmid, acc, sec, drow, prod, fin, done, sem):
         tm = where_ref[0]
         rw = where_ref[1]
         lat[...] = jnp.zeros_like(lat)
@@ -139,7 +142,7 @@
         r_odd = rw % 2 == 1
         t_odd = tm % 2 == 1
         for bo in range(4):
-            other_c = 1 - bo % 2
+            own, za, zb = (own0, za0, zb0) if bo % 2 else (own1, za1, zb1)
             if bo == 3:
                 dx = 0
             elif bo == 2:
@@ -167,7 +170,7 @@
                         h = 2 * (ro + 2) + row - 1
                         n = 2 * f + row
                         for tile in (n, 4):
-                            at = (y, dx, other_c, tile)
+                            at = (y, dx, tile)
                             if ro == 0:
                                 v = own[at]
                             else:
@@ -287,12 +290,12 @@
     w_entry, w_mid = pl.pallas_call(
         prepare_middle,
         out_shape=(VM((3, 3 * ch, ch), BF), VM((16, 3 * ch, ch), BF)),
-        in_specs=[vmem, hbm],
+        in_specs=[hbm, hbm],
         out_specs=(vmem, vmem),
-        scratch_shapes=fetched,
+        scratch_shapes=fetched + [VM((27 * cin, ch), BF), pltpu.SemaphoreType.DMA(())],
         compiler_params=small,
         name="prepare_middle",
-    )(entry_kernel.reshape(27 * cin, ch), keep(middle_kernel.reshape(27, ch, ch)))
+    )(keep(entry_kernel.reshape(27 * cin, ch)), keep(middle_kernel.reshape(27, ch, ch)))
     w_up = pl.pallas_call(
         prepare_upper,
         out_shape=VM((9, 3 * ch, ch), BF),
@@ -311,8 +314,6 @@
         compiler_params=small,
         name="pack",
     )(x)
-    other = swap(x, "tm", 1)
-    x = jnp.stack([x, other])
     steps = [d for d in (2, 4) if d < n_tm]
     others = [lax.ppermute(x, "tm", [(i, (i + d) % n_tm) for i in range(n_tm)]) for d in steps]
     x = jnp.stack([x] + others)
@@ -320,12 +321,13 @@
     x = jnp.stack([x, other])
     za = swap(x, "rows", 2)
     zb = swap_across(x, "rows")
+    both = [(v, swap(v, "tm", 1)) for v in (x, za, zb)]
     where = jnp.stack([lax.axis_index("tm"), lax.axis_index("rows")]).astype(jnp.int32)
     kernel = make_main(n_rows, cin, width, ch, 1 + len(steps))
     return pl.pallas_call(
         kernel,
         out_shape=jax.ShapeDtypeStruct((frames, 2 * height, 2 * width, ch), BF),
-        in_specs=[pl.BlockSpec(memory_space=pltpu.SMEM)] + [vmem] * 6,
+        in_specs=[pl.BlockSpec(memory_space=pltpu.SMEM)] + [vmem] * 9,
         out_specs=pl.BlockSpec(memory_space=pl.ANY),
         scratch_shapes=[
             VM((8, 8 * cin, -(-width // 128) * 128), BF),
@@ -340,9 +342,9 @@
             VM((8, 2 * width, ch), BF),
             pltpu.SemaphoreType.DMA((8,)),
         ],
-        compiler_params=pltpu.CompilerParams(vmem_limit_bytes=32 * 2**20),
+        compiler_params=pltpu.CompilerParams(vmem_limit_bytes=26 * 2**20),
         name="section",
-    )(where, x, za, zb, w_entry, w_mid, w_up)
+    )(where, *both[0], *both[1], *both[2], w_entry, w_mid, w_up)
 
 
 def solution(mesh):

time: 34 us -> 33.9 us (level)
  waiting for transfers between devices: 5.25 us -> 4.86 us
    ppermute x3 -> x5, waiting for transfers between devices: 3.27 us -> 3.1 us  [swap(): return lax.ppermute(block, axis, [(i, i ^ distance) for i in range(size)])]
    ppermute x3 -> x5, starting transfers between devices: 7.57 us -> 7.72 us  [swap(): return lax.ppermute(block, axis, [(i, i ^ distance) for i in range(size)])]
    unnamed x4 -> x2, local copies, waits for them, and re-layouts: 0.76 us -> 0.76 us
  transfers between devices with their start and end apart: 5 -> 7, of which waited for: 3 -> 5; matrix products, arithmetic and copies ran while one was open for 0% -> 0% of each run, Pallas kernels for 14% -> 15%
where the time goes in v3:
time: 33.9 us; the launch traced here: 33.7 us
  Pallas kernels  16.6 us (49%)
  starting transfers between devices  11.4 us (34%)
  waiting for transfers between devices  4.86 us (14%)
  local copies, waits for them, and re-layouts  0.76 us (2%)
    pallas_call x1, Pallas kernels, per_device(): pl.pallas_call(kernel, out_shape=jax.ShapeDtypeStruct((frames, 2 * height...  11.6 us
    ppermute x5, starting transfers between devices, swap(): return lax.ppermute(block, axis, [(i, i ^ distance) for i in range(size)])  7.72 us
    ppermute x5, waiting for transfers between devices, swap(): return lax.ppermute(block, axis, [(i, i ^ distance) for i in range(size)])  3.1 us
    ppermute x1, starting transfers between devices, per_device(): lax.ppermute(x, 'tm', [(i, (i + d) % n_tm) for i in range(n_tm)])  2.97 us
    pallas_call x1, Pallas kernels, per_device(): pl.pallas_call(prepare_middle, out_shape=(VM((3, 3 * ch, ch), BF), VM((16...  2.71 us
    pallas_call x1, Pallas kernels, per_device(): pl.pallas_call(prepare_upper, out_shape=VM((9, 3 * ch, ch), BF), in_specs...  2.22 us
    ppermute x1, waiting for transfers between devices, per_device(): lax.ppermute(x, 'tm', [(i, (i + d) % n_tm) for i in range(n_tm)])  1.76 us
    unnamed x2, local copies, waits for them, and re-layouts  0.76 us
  transfers between devices with their start and end apart: 7, of which 5 were waited for; matrix products, arithmetic and copies ran while one was open for 0% of the time, Pallas kernels for 15%

profile of v3, /device:TPU:0, one launch (start us, length us, event | category | flops | bytes accessed | tf_op | source)
XLA Modules:
  0.0 33.7 jit_solution(4912276957923864535)
XLA Ops:
  0.0 0.0 copy-start
  0.0 0.8 %copy-done = bf16[2,2,160,16]{2,3,1,0:T(8,128)(2,1)S(1)} copy-done((bf16[2,2,160,16]{2,3,1,0:T(8,128)(2,1)S(1)}, bf16[2,2,160,16]{2,3,1,0:T(8,128)(2,1)}, u32[]{:S(2)}) %copy-start) | copy-done | bytes 20504
  0.8 0.1 pack.1
  0.8 3.0 %collective-permute-start = (bf16[5,16,128]{2,1,0:T(8,128)(2,1)S(1)}, bf16[5,16,128]{2,1,0:T(8,128)(2,1)S(1)}, u32[]{:S(2)}, u32[]{:S(2)}) collective-permute-start(bf16[5,16,128]{2,1,0:T(8,128)(2,1)S(1)} %pack.1), channel_id=1, source_target_pairs={{0,16},{8,24},{16,0},{24,8},{1,17},{9,25},{17,1},{25,9},{2,18},{10... | collective-permute-start | bytes 61448 | tf_op jit(solution)/shard_map/ppermute | solution.py:318
  3.8 1.8 %collective-permute-done = bf16[5,16,128]{2,1,0:T(8,128)(2,1)S(1)} collective-permute-done((bf16[5,16,128]{2,1,0:T(8,128)(2,1)S(1)}, bf16[5,16,128]{2,1,0:T(8,128)(2,1)S(1)}, u32[]{:S(2)}, u32[]{:S(2)}) %collective-permute-start) | collective-permute-done | bytes 20512 | tf_op jit(solution)/shard_map/ppermute | solution.py:318
  5.6 2.1 %collective-permute-start.1 = (bf16[2,5,16,128]{3,2,1,0:T(8,128)(2,1)S(1)}, bf16[2,5,16,128]{3,2,1,0:T(8,128)(2,1)S(1)}, u32[]{:S(2)}, u32[]{:S(2)}) collective-permute-start(bf16[2,5,16,128]{3,2,1,0:T(8,128)(2,1)S(1)} %get-tuple-element.10), channel_id=1, source_target_pairs={{0,1},{1,0},{2,3},{3,2},{4,5},{5,4},{6,7},{7,6},{8,9},{9,8},{10,11... | collective-permute-start | bytes 122888 | tf_op jit(solution)/shard_map/ppermute | solution.py:18
  7.7 2.0 %collective-permute-done.1 = bf16[2,5,16,128]{3,2,1,0:T(8,128)(2,1)S(1)} collective-permute-done((bf16[2,5,16,128]{3,2,1,0:T(8,128)(2,1)S(1)}, bf16[2,5,16,128]{3,2,1,0:T(8,128)(2,1)S(1)}, u32[]{:S(2)}, u32[]{:S(2)}) %collective-permute-start.1) | collective-permute-done | bytes 40992 | tf_op jit(solution)/shard_map/ppermute | solution.py:18
  9.7 0.7 %collective-permute-start.5 = (bf16[2,2,5,16,128]{4,3,2,1,0:T(8,128)(2,1)S(1)}, bf16[2,2,5,16,128]{4,3,2,1,0:T(8,128)(2,1)S(1)}, u32[]{:S(2)}, u32[]{:S(2)}) collective-permute-start(bf16[2,2,5,16,128]{4,3,2,1,0:T(8,128)(2,1)S(1)} %pad_maximum_fusion.own0), channel_id=1, source_target_pairs={{2,4},{3,5},{4,2},{5,3},{10,12},{11,13},{12,10},{13,11},{18,20},{1... | collective-permute-start | bytes 245768 | tf_op jit(solution)/shard_map/ppermute | solution.py:28
  10.4 5.0 %collective-permute-start.3 = (bf16[2,2,5,16,128]{4,3,2,1,0:T(8,128)(2,1)S(1)}, bf16[2,2,5,16,128]{4,3,2,1,0:T(8,128)(2,1)S(1)}, u32[]{:S(2)}, u32[]{:S(2)}) collective-permute-start(bf16[2,2,5,16,128]{4,3,2,1,0:T(8,128)(2,1)S(1)} %pad_maximum_fusion.own0), channel_id=1, source_target_pairs={{0,2},{1,3},{2,0},{3,1},{4,6},{5,7},{6,4},{7,5},{8,10},{9,11},{10,... | collective-permute-start | bytes 245768 | tf_op jit(solution)/shard_map/ppermute | solution.py:18
  15.3 2.2 %prepare_upper.1.w_up = bf16[9,768,256]{2,1,0:T(8,128)(2,1)S(1)} custom-call(bf16[27,256,256]{2,1,0:T(8,128)(2,1)} %bitcast.15), custom_call_target="tpu_custom_call" | custom-call | tf_op jit(solution)/shard_map/prepare_upper/pallas_call | solution.py:299
  17.5 2.7 %prepare_middle.1 = (bf16[3,768,256]{2,1,0:T(8,128)(2,1)S(1)}, bf16[16,768,256]{2,1,0:T(8,128)(2,1)S(1)}) custom-call(bf16[432,256]{1,0:T(8,128)(2,1)} %bitcast.17, bf16[27,256,256]{2,1,0:T(8,128)(2,1)} %bitcast.16), custom_call_target="tpu_custom_call" | custom-call | tf_op jit(solution)/shard_map/prepare_middle/pallas_call | solution.py:290
  20.3 0.1 collective-permute-start.2
  20.3 0.0 collective-permute-done.5.zb0
  20.4 0.5 %collective-permute-start.6 = (bf16[2,2,5,16,128]{4,3,2,1,0:T(8,128)(2,1)S(1)}, bf16[2,2,5,16,128]{4,3,2,1,0:T(8,128)(2,1)S(1)}, u32[]{:S(2)}, u32[]{:S(2)}) collective-permute-start(bf16[2,2,5,16,128]{4,3,2,1,0:T(8,128)(2,1)S(1)} %collective-permute-done.5.zb0), channel_id=1, source_target_pairs={{0,8},{8,0},{16,24},{24,16},{1,9},{9,1},{17,25},{25,17},{2,10},{10... | collective-permute-start | bytes 245768 | tf_op jit(solution)/shard_map/ppermute | solution.py:18
  20.8 0.0 collective-permute-done.3.za0
  20.8 0.1 collective-permute-start.4
  20.9 0.1 pad_add_fusion.where_ref
  21.0 0.6 %collective-permute-done.2.own1 = bf16[2,2,5,16,128]{4,3,2,1,0:T(8,128)(2,1)S(1)} collective-permute-done((bf16[2,2,5,16,128]{4,3,2,1,0:T(8,128)(2,1)S(1)}, bf16[2,2,5,16,128]{4,3,2,1,0:T(8,128)(2,1)S(1)}, u32[]{:S(2)}, u32[]{:S(2)}) %collective-permute-start.2) | collective-permute-done | bytes 81952 | tf_op jit(solution)/shard_map/ppermute | solution.py:18
  21.6 0.2 collective-permute-done.6.zb1
  21.8 0.4 %collective-permute-done.4.za1 = bf16[2,2,5,16,128]{4,3,2,1,0:T(8,128)(2,1)S(1)} collective-permute-done((bf16[2,2,5,16,128]{4,3,2,1,0:T(8,128)(2,1)S(1)}, bf16[2,2,5,16,128]{4,3,2,1,0:T(8,128)(2,1)S(1)}, u32[]{:S(2)}, u32[]{:S(2)}) %collective-permute-start.4) | collective-permute-done | bytes 81952 | tf_op jit(solution)/shard_map/ppermute | solution.py:18
  22.1 11.6 %section.1 = bf16[2,4,320,256]{3,2,1,0:T(8,128)(2,1)} custom-call(s32[2]{0:T(128)S(1)} %pad_add_fusion.where_ref, bf16[2,2,5,16,128]{4,3,2,1,0:T(8,128)(2,1)S(1)} %pad_maximum_fusion.own0, bf16[2,2,5,16,128]{4,3,2,1,0:T(8,128)(2,1)S(1)} %collective-permute-done.2.own1, bf16[2,2,5,16,128]{4,3,2,1,0:T(8,128)(2,1)S(1)} %collective-permute-done.3.za0, ...), custom_call_target="tpu_custom_call" | custom-call | tf_op jit(solution)/shard_map/section/pallas_call | solution.py:327
  (2 shorter events, 0.0 us)
Async XLA Ops:
  0.0 0.8 %copy-start = (bf16[2,2,160,16]{2,3,1,0:T(8,128)(2,1)S(1)}, bf16[2,2,160,16]{2,3,1,0:T(8,128)(2,1)}, u32[]{:S(2)}) copy-start(bf16[2,2,160,16]{2,3,1,0:T(8,128)(2,1)} %param.4) | copy-start | bytes 61444
  0.8 4.7 %collective-permute-start = (bf16[5,16,128]{2,1,0:T(8,128)(2,1)S(1)}, bf16[5,16,128]{2,1,0:T(8,128)(2,1)S(1)}, u32[]{:S(2)}, u32[]{:S(2)}) collective-permute-start(bf16[5,16,128]{2,1,0:T(8,128)(2,1)S(1)} %pack.1), channel_id=1, source_target_pairs={{0,16},{8,24},{16,0},{24,8},{1,17},{9,25},{17,1},{25,9},{2,18},{10... | collective-permute-start | bytes 61448 | tf_op jit(solution)/shard_map/ppermute | solution.py:318
  5.6 4.1 %collective-permute-start.1 = (bf16[2,5,16,128]{3,2,1,0:T(8,128)(2,1)S(1)}, bf16[2,5,16,128]{3,2,1,0:T(8,128)(2,1)S(1)}, u32[]{:S(2)}, u32[]{:S(2)}) collective-permute-start(bf16[2,5,16,128]{3,2,1,0:T(8,128)(2,1)S(1)} %get-tuple-element.10), channel_id=1, source_target_pairs={{0,1},{1,0},{2,3},{3,2},{4,5},{5,4},{6,7},{7,6},{8,9},{9,8},{10,11... | collective-permute-start | bytes 122888 | tf_op jit(solution)/shard_map/ppermute | solution.py:18
  9.7 10.7 %collective-permute-start.5 = (bf16[2,2,5,16,128]{4,3,2,1,0:T(8,128)(2,1)S(1)}, bf16[2,2,5,16,128]{4,3,2,1,0:T(8,128)(2,1)S(1)}, u32[]{:S(2)}, u32[]{:S(2)}) collective-permute-start(bf16[2,2,5,16,128]{4,3,2,1,0:T(8,128)(2,1)S(1)} %pad_maximum_fusion.own0), channel_id=1, source_target_pairs={{2,4},{3,5},{4,2},{5,3},{10,12},{11,13},{12,10},{13,11},{18,20},{1... | collective-permute-start | bytes 245768 | tf_op jit(solution)/shard_map/ppermute | solution.py:28
  10.4 10.5 %collective-permute-start.3 = (bf16[2,2,5,16,128]{4,3,2,1,0:T(8,128)(2,1)S(1)}, bf16[2,2,5,16,128]{4,3,2,1,0:T(8,128)(2,1)S(1)}, u32[]{:S(2)}, u32[]{:S(2)}) collective-permute-start(bf16[2,2,5,16,128]{4,3,2,1,0:T(8,128)(2,1)S(1)} %pad_maximum_fusion.own0), channel_id=1, source_target_pairs={{0,2},{1,3},{2,0},{3,1},{4,6},{5,7},{6,4},{7,5},{8,10},{9,11},{10,... | collective-permute-start | bytes 245768 | tf_op jit(solution)/shard_map/ppermute | solution.py:18
  20.3 1.3 %collective-permute-start.2 = (bf16[2,2,5,16,128]{4,3,2,1,0:T(8,128)(2,1)S(1)}, bf16[2,2,5,16,128]{4,3,2,1,0:T(8,128)(2,1)S(1)}, u32[]{:S(2)}, u32[]{:S(2)}) collective-permute-start(bf16[2,2,5,16,128]{4,3,2,1,0:T(8,128)(2,1)S(1)} %pad_maximum_fusion.own0), channel_id=1, source_target_pairs={{0,8},{8,0},{16,24},{24,16},{1,9},{9,1},{17,25},{25,17},{2,10},{10... | collective-permute-start | bytes 245768 | tf_op jit(solution)/shard_map/ppermute | solution.py:18
  20.4 1.4 %collective-permute-start.6 = (bf16[2,2,5,16,128]{4,3,2,1,0:T(8,128)(2,1)S(1)}, bf16[2,2,5,16,128]{4,3,2,1,0:T(8,128)(2,1)S(1)}, u32[]{:S(2)}, u32[]{:S(2)}) collective-permute-start(bf16[2,2,5,16,128]{4,3,2,1,0:T(8,128)(2,1)S(1)} %collective-permute-done.5.zb0), channel_id=1, source_target_pairs={{0,8},{8,0},{16,24},{24,16},{1,9},{9,1},{17,25},{25,17},{2,10},{10... | collective-permute-start | bytes 245768 | tf_op jit(solution)/shard_map/ppermute | solution.py:18
  20.8 1.3 %collective-permute-start.4 = (bf16[2,2,5,16,128]{4,3,2,1,0:T(8,128)(2,1)S(1)}, bf16[2,2,5,16,128]{4,3,2,1,0:T(8,128)(2,1)S(1)}, u32[]{:S(2)}, u32[]{:S(2)}) collective-permute-start(bf16[2,2,5,16,128]{4,3,2,1,0:T(8,128)(2,1)S(1)} %collective-permute-done.3.za0), channel_id=1, source_target_pairs={{0,8},{8,0},{16,24},{24,16},{1,9},{9,1},{17,25},{25,17},{2,10},{10... | collective-permute-start | bytes 245768 | tf_op jit(solution)/shard_map/ppermute | solution.py:18
